TPU v7x, 256 devices: a whole 4x4x8 slice. The times are simulated.
256 devices in a mesh: dp: 8 (over z_lo, y), expert: 32 (over z_hi, x, core).
Axes of the slice: x: 4, y: 4, z: 8 (z_hi: 4, z_lo: 2; z = z_hi * 2 + z_lo), core: 2. Of those that a mesh axis runs over, the one named last changes fastest.
Arguments:
- cell_rows: bfloat16 [2, 32768, 1024], P(None, ('dp', 'expert')), may hold values from -24 to 24
- cotangent: bfloat16 [2, 32768, 1024], P(None, ('dp', 'expert')), may hold values from -0.75 to 0.75
- cluster_ids: int32 [2, 32768, 1], P(None, ('dp', 'expert')), may hold values from 0 to 31; in each aligned block of 128 rows (0 to 127, 128 to 255, ..., all dimensions but the last counted through in order) at most 8 rows name the same one
- enc_weight: bfloat16 [1024, 1024], replicated, may hold values from -0.1875 to 0.1875
- up_weight: bfloat16 [32, 1024, 2048], P('expert'), may hold values from -0.1875 to 0.1875
- down_weight: bfloat16 [32, 1024, 2048], P('expert'), may hold values from -0.125 to 0.125
Outputs:
- enc_grad: float32 [1024, 1024], P(('dp', 'expert'))
- up_grad: bfloat16 [32, 1024, 2048], P('expert', 'dp')
- down_grad: bfloat16 [32, 1024, 2048], P('expert', 'dp')
Inputs may be any that keep to these rules, and one draw needn't show every extreme that they name: `cluster_ids`: in each micro-batch the 128 rows of one device name one cluster at most 8 times, a bound that some block reaches.
All inputs are finite; a program needn't handle non-finite values.
Results may differ from a plain program's by a relative error of at most 0.014.
Values may be sent and summed in bfloat16 or wider, within the bound.
A program may use at most 128 MiB of HBM per device.

v0:
```python
import jax
import jax.numpy as jnp
from jax import lax
from jax.sharding import PartitionSpec as P

epsilon = 1e-06
contract_rows = (((0,), (0,)), ((), ()))


def silu_pair(pre_value):
    gate_value = jax.nn.sigmoid(pre_value)
    return (pre_value * gate_value, gate_value * (1.0 + pre_value * (1.0 - gate_value)))


def body(cell_rows, cotangent, cluster_ids, enc_weight, up_weight, down_weight):
    experts = lax.axis_size("expert")
    dp_count = lax.axis_size("dp")
    batch_count, local_rows, model_width = cell_rows.shape
    capacity = max(2, local_rows // 16)
    slot_count = experts * capacity
    w_up = up_weight[0]
    w_down = down_weight[0]
    hidden_width = w_up.shape[1]
    up_running = jnp.zeros((model_width, hidden_width), jnp.float32)
    down_running = jnp.zeros((model_width, hidden_width), jnp.float32)
    encoder_pieces = []
    for batch_index in range(batch_count):
        features = cell_rows[batch_index]
        grad_out = cotangent[batch_index]
        pre_enc = jnp.dot(features, enc_weight, preferred_element_type=jnp.float32)
        silu_enc, slope_enc = silu_pair(pre_enc)
        encoded = features.astype(jnp.float32) + silu_enc
        inverse = lax.rsqrt(jnp.mean(encoded * encoded, axis=1, keepdims=True) + epsilon)
        normed = (encoded * inverse).astype(jnp.bfloat16)
        labels = cluster_ids[batch_index, :, 0]
        onehot = (labels[:, None] == jnp.arange(experts, dtype=jnp.int32)[None, :]).astype(
            jnp.int32
        )
        slot_rank = jnp.sum((jnp.cumsum(onehot, axis=0) - onehot) * onehot, axis=1)
        target = labels * capacity + slot_rank
        placer = (jnp.arange(slot_count, dtype=jnp.int32)[:, None] == target[None, :]).astype(
            jnp.bfloat16
        )
        send_norm = jnp.dot(placer, normed, preferred_element_type=jnp.float32).astype(jnp.bfloat16)
        send_grad = jnp.dot(placer, grad_out, preferred_element_type=jnp.float32).astype(
            jnp.bfloat16
        )
        recv_norm, recv_grad = (
            lax.all_to_all(
                send_norm.reshape(experts, capacity, model_width),
                "expert",
                split_axis=0,
                concat_axis=0,
                tiled=True,
            ),
            lax.all_to_all(
                send_grad.reshape(experts, capacity, model_width),
                "expert",
                split_axis=0,
                concat_axis=0,
                tiled=True,
            ),
        )
        norm_rows = recv_norm.reshape(slot_count, model_width)
        grad_rows = recv_grad.reshape(slot_count, model_width)
        pre_exp = jnp.dot(norm_rows, w_up, preferred_element_type=jnp.float32)
        silu_exp, slope_exp = silu_pair(pre_exp)
        active = silu_exp.astype(jnp.bfloat16)
        act_grad = jnp.dot(grad_rows, w_down, preferred_element_type=jnp.float32)
        pre_grad = (act_grad * slope_exp).astype(jnp.bfloat16)
        back_rows = lax.dot_general(
            pre_grad, w_up, (((1,), (1,)), ((), ())), preferred_element_type=jnp.float32
        ).astype(jnp.bfloat16)
        returned = lax.all_to_all(
            back_rows.reshape(experts, capacity, model_width),
            "expert",
            split_axis=0,
            concat_axis=0,
            tiled=True,
        )
        norm_grad = lax.dot_general(
            placer,
            returned.reshape(slot_count, model_width),
            contract_rows,
            preferred_element_type=jnp.float32,
        )
        enc_rows_grad = inverse * norm_grad - inverse * inverse * inverse * encoded * jnp.mean(
            norm_grad * encoded, axis=1, keepdims=True
        )
        enc_pre_grad = (enc_rows_grad * slope_enc).astype(jnp.bfloat16)
        encoder_pieces.append((features, enc_pre_grad))
        up_running = up_running + lax.dot_general(
            norm_rows, pre_grad, contract_rows, preferred_element_type=jnp.float32
        )
        down_running = down_running + lax.dot_general(
            grad_rows, active, contract_rows, preferred_element_type=jnp.float32
        )
    up_sum, down_sum = (
        lax.psum_scatter(
            up_running.astype(jnp.bfloat16), "dp", scatter_dimension=0, tiled=True
        ).astype(jnp.float32),
        lax.psum_scatter(
            down_running.astype(jnp.bfloat16), "dp", scatter_dimension=0, tiled=True
        ).astype(jnp.float32),
    )
    enc_share = model_width // (dp_count * experts)
    running = jnp.zeros((lax.axis_size(("dp", "expert")) * enc_share, model_width), jnp.float32)
    for features, enc_pre_grad in encoder_pieces:
        running = running + lax.dot_general(
            features, enc_pre_grad, contract_rows, preferred_element_type=jnp.float32
        )
    enc_sum = lax.psum_scatter(running, ("dp", "expert"), scatter_dimension=0, tiled=True)
    return (enc_sum, up_sum.astype(jnp.bfloat16)[None], down_sum.astype(jnp.bfloat16)[None])


def solution(mesh):
    in_specs = (
        P(None, ("dp", "expert"), None),
        P(None, ("dp", "expert"), None),
        P(None, ("dp", "expert"), None),
        P(),
        P("expert", None, None),
        P("expert", None, None),
    )
    out_specs = (P(("dp", "expert"), None), P("expert", "dp", None), P("expert", "dp", None))
    return jax.shard_map(body, mesh=mesh, in_specs=in_specs, out_specs=out_specs, check_vma=False)
```

profile of v0, /device:TPU:1, one launch (start us, length us, event | category | flops | bytes accessed | tf_op | source)
XLA Modules:
  0.0 482.3 jit_solution(4993714192760767541)
XLA Ops:
  8.0 0.0 copy-start
  8.0 0.0 copy-start.1
  8.0 0.8 slice_bitcast_fusion
  8.9 0.1 fusion.84
  8.9 0.1 fusion.88
  9.0 0.2 reduce_window_sum.18
  9.2 0.2 reduce_window_sum.17
  9.4 0.2 copy-done
  9.6 1.4 fusion.63
  11.0 0.0 copy-done.1
  11.0 0.0 copy-start.6
  11.0 0.0 copy-start.13
  11.1 1.4 multiply_reduce_fusion.1
  12.5 0.2 select_reduce_fusion
  12.7 0.0 copy-done.13
  12.7 1.2 fusion.31
  13.9 12.6 %all-to-all-start.1 = ((bf16[32,8,1024]{2,1,0:T(8,128)(2,1)}), bf16[32,8,1024]{2,1,0:T(8,128)(2,1)S(1)}, u32[]{:S(2)}, u32[]{:S(2)}) async-start(bf16[32,8,1024]{2,1,0:T(8,128)(2,1)} %fusion.31), calls=%async_computation.1 | async-start | bytes 1048576 | tf_op jit(solution)/shard_map/all_to_all | solution.py:49
  26.5 2.2 fusion.33
  28.7 15.9 %all-to-all-done.1 = bf16[32,8,1024]{2,1,0:T(8,128)(2,1)S(1)} async-done(((bf16[32,8,1024]{2,1,0:T(8,128)(2,1)}), bf16[32,8,1024]{2,1,0:T(8,128)(2,1)S(1)}, u32[]{:S(2)}, u32[]{:S(2)}) %all-to-all-start.1) | async-done | bytes 524320 | tf_op jit(solution)/shard_map/all_to_all | solution.py:49
  44.6 0.8 copy-done.2
  45.4 4.2 all-to-all-start.4
  49.7 2.0 fusion.30
  51.7 15.2 %all-to-all-done.4 = bf16[32,8,1024]{2,1,0:T(8,128)(2,1)S(1)} async-done(((bf16[32,8,1024]{2,1,0:T(8,128)(2,1)}), bf16[32,8,1024]{2,1,0:T(8,128)(2,1)S(1)}, u32[]{:S(2)}, u32[]{:S(2)}) %all-to-all-start.4) | async-done | bytes 524320 | tf_op jit(solution)/shard_map/all_to_all | solution.py:49
  66.9 5.3 %all-to-all-start = ((bf16[32,8,1024]{2,1,0:T(8,128)(2,1)}), bf16[32,8,1024]{2,1,0:T(8,128)(2,1)}, u32[]{:S(2)}, u32[]{:S(2)}) async-start(bf16[32,8,1024]{2,1,0:T(8,128)(2,1)} %fusion.30), calls=%async_computation | async-start | bytes 1048576 | tf_op jit(solution)/shard_map/all_to_all | solution.py:56
  72.2 2.0 fusion.32
  74.2 5.0 %fusion.2 = f32[256,2048]{1,0:T(8,128)} fusion(bf16[1,1024,2048]{2,1,0:T(8,128)(2,1)} %param.10, bf16[32,8,1024]{2,1,0:T(8,128)(2,1)S(1)} %all-to-all-done.4), kind=kOutput, calls=%fused_computation.4 | convolution fusion | flops 1073741824 | bytes 6815744 | tf_op jit(solution)/shard_map/dot_general | solution.py:66
  79.2 2.6 fusion.6
  81.8 7.3 %all-to-all-done = bf16[32,8,1024]{2,1,0:T(8,128)(2,1)} async-done(((bf16[32,8,1024]{2,1,0:T(8,128)(2,1)}), bf16[32,8,1024]{2,1,0:T(8,128)(2,1)}, u32[]{:S(2)}, u32[]{:S(2)}) %all-to-all-start) | async-done | bytes 524320 | tf_op jit(solution)/shard_map/all_to_all | solution.py:56
  89.1 5.8 %all-to-all-start.3 = ((bf16[32,8,1024]{2,1,0:T(8,128)(2,1)}), bf16[32,8,1024]{2,1,0:T(8,128)(2,1)}, u32[]{:S(2)}, u32[]{:S(2)}) async-start(bf16[32,8,1024]{2,1,0:T(8,128)(2,1)} %fusion.32), calls=%async_computation.3 | async-start | bytes 1048576 | tf_op jit(solution)/shard_map/all_to_all | solution.py:56
  95.0 0.0 copy-start.15
  95.0 4.6 fusion.21
  99.5 0.0 copy-start.9
  99.6 1.1 copy-done.9
  100.6 2.1 fusion.37
  102.7 9.1 %all-to-all-done.3 = bf16[32,8,1024]{2,1,0:T(8,128)(2,1)} async-done(((bf16[32,8,1024]{2,1,0:T(8,128)(2,1)}), bf16[32,8,1024]{2,1,0:T(8,128)(2,1)}, u32[]{:S(2)}, u32[]{:S(2)}) %all-to-all-start.3) | async-done | bytes 524320 | tf_op jit(solution)/shard_map/all_to_all | solution.py:56
  111.7 6.0 %all-to-all-start.2 = ((bf16[32,8,1024]{2,1,0:T(8,128)(2,1)}), bf16[32,8,1024]{2,1,0:T(8,128)(2,1)}, u32[]{:S(2)}, u32[]{:S(2)}) async-start(bf16[32,8,1024]{2,1,0:T(8,128)(2,1)} %fusion.37), calls=%async_computation.2 | async-start | bytes 1048576 | tf_op jit(solution)/shard_map/all_to_all | solution.py:74
  117.7 0.0 copy-start.16
  117.7 4.6 fusion.18
  122.3 0.0 copy-start.10
  122.3 1.0 copy-done.10
  123.3 2.1 fusion.34
  125.4 9.1 %all-to-all-done.2 = bf16[32,8,1024]{2,1,0:T(8,128)(2,1)} async-done(((bf16[32,8,1024]{2,1,0:T(8,128)(2,1)}), bf16[32,8,1024]{2,1,0:T(8,128)(2,1)}, u32[]{:S(2)}, u32[]{:S(2)}) %all-to-all-start.2) | async-done | bytes 524320 | tf_op jit(solution)/shard_map/all_to_all | solution.py:74
  134.5 6.0 %all-to-all-start.5 = ((bf16[32,8,1024]{2,1,0:T(8,128)(2,1)}), bf16[32,8,1024]{2,1,0:T(8,128)(2,1)}, u32[]{:S(2)}, u32[]{:S(2)}) async-start(bf16[32,8,1024]{2,1,0:T(8,128)(2,1)} %fusion.34), calls=%async_computation.5 | async-start | bytes 1048576 | tf_op jit(solution)/shard_map/all_to_all | solution.py:74
  140.5 0.0 all-reduce.3.cloned.1.call-start
  140.5 2.1 fusion.49
  142.7 14.6 %all-to-all-done.5 = bf16[32,8,1024]{2,1,0:T(8,128)(2,1)} async-done(((bf16[32,8,1024]{2,1,0:T(8,128)(2,1)}), bf16[32,8,1024]{2,1,0:T(8,128)(2,1)}, u32[]{:S(2)}, u32[]{:S(2)}) %all-to-all-start.5) | async-done | bytes 524320 | tf_op jit(solution)/shard_map/all_to_all | solution.py:74
  157.3 2.2 multiply_reduce_fusion
  159.5 0.0 copy-start.12
  159.5 0.9 fusion.56
  160.4 0.1 copy-done.12
  160.5 2.9 add_bitcast_fusion
  163.4 0.0 all-reduce.3.cloned.1.call-update
  163.5 0.0 reduce-scatter.6.cloned.1.call-start
  163.5 3.3 fusion.40
  166.8 4.4 add_convert_fusion
  171.3 0.0 reduce-scatter.6.cloned.1.call-update
  171.3 0.0 reduce-scatter.4.cloned.1.call-start
  171.3 1.0 copy-done.4
  172.3 2.6 fusion.51
  175.0 3.2 add_convert_fusion.1
  178.2 0.0 reduce-scatter.4.cloned.1.call-update
  178.2 294.6 %all-reduce.3.cloned.1.call-done = f32[1024,1024]{0,1:T(8,128)} async-done(((f32[1024,1024]{0,1:T(8,128)}), f32[1024,1024]{0,1:T(8,128)}) %all-reduce.3.cloned.1.call-update) | async-done | bytes 4194320
  472.8 1.2 constant_dynamic-slice_fusion
  474.1 0.8 copy.10
  (24 shorter events, 0.1 us)
Async XLA Ops:
  8.0 1.6 copy-start
  8.0 3.0 copy-start.1
  11.0 1.7 copy-start.6
  11.0 1.6 copy-start.13
  13.9 30.7 %all-to-all-start.1 = ((bf16[32,8,1024]{2,1,0:T(8,128)(2,1)}), bf16[32,8,1024]{2,1,0:T(8,128)(2,1)S(1)}, u32[]{:S(2)}, u32[]{:S(2)}) async-start(bf16[32,8,1024]{2,1,0:T(8,128)(2,1)} %fusion.31), calls=%async_computation.1 | async-start | bytes 1048576 | tf_op jit(solution)/shard_map/all_to_all | solution.py:49
  44.6 0.8 copy-start.2
  45.4 21.5 %all-to-all-start.4 = ((bf16[32,8,1024]{2,1,0:T(8,128)(2,1)}), bf16[32,8,1024]{2,1,0:T(8,128)(2,1)S(1)}, u32[]{:S(2)}, u32[]{:S(2)}) async-start(bf16[32,8,1024]{2,1,0:T(8,128)(2,1)} %fusion.33), calls=%async_computation.4 | async-start | bytes 1048576 | tf_op jit(solution)/shard_map/all_to_all | solution.py:49
  66.9 22.2 %all-to-all-start = ((bf16[32,8,1024]{2,1,0:T(8,128)(2,1)}), bf16[32,8,1024]{2,1,0:T(8,128)(2,1)}, u32[]{:S(2)}, u32[]{:S(2)}) async-start(bf16[32,8,1024]{2,1,0:T(8,128)(2,1)} %fusion.30), calls=%async_computation | async-start | bytes 1048576 | tf_op jit(solution)/shard_map/all_to_all | solution.py:56
  74.2 5.0 %copy-start.3 = (bf16[32,8,1024]{2,1,0:T(8,128)(2,1)S(1)}, bf16[32,8,1024]{2,1,0:T(8,128)(2,1)}, u32[]{:S(2)}) copy-start(bf16[32,8,1024]{2,1,0:T(8,128)(2,1)} %copy-done.2) | copy-start | bytes 1572868
  74.2 5.0 %copy-start.14 = (bf16[1,1024,2048]{2,1,0:T(8,128)(2,1)S(1)}, bf16[1,1024,2048]{2,1,0:T(8,128)(2,1)}, u32[]{:S(2)}) copy-start(bf16[1,1024,2048]{2,1,0:T(8,128)(2,1)} %param.10) | copy-start | bytes 12582916
  89.1 22.6 %all-to-all-start.3 = ((bf16[32,8,1024]{2,1,0:T(8,128)(2,1)}), bf16[32,8,1024]{2,1,0:T(8,128)(2,1)}, u32[]{:S(2)}, u32[]{:S(2)}) async-start(bf16[32,8,1024]{2,1,0:T(8,128)(2,1)} %fusion.32), calls=%async_computation.3 | async-start | bytes 1048576 | tf_op jit(solution)/shard_map/all_to_all | solution.py:56
  95.0 5.6 %copy-start.15 = (bf16[1,1024,2048]{2,1,0:T(8,128)(2,1)S(1)}, bf16[1,1024,2048]{2,1,0:T(8,128)(2,1)}, u32[]{:S(2)}) copy-start(bf16[1,1024,2048]{2,1,0:T(8,128)(2,1)} %param.10) | copy-start | bytes 12582916
  99.5 1.1 copy-start.9
  111.7 22.8 %all-to-all-start.2 = ((bf16[32,8,1024]{2,1,0:T(8,128)(2,1)}), bf16[32,8,1024]{2,1,0:T(8,128)(2,1)}, u32[]{:S(2)}, u32[]{:S(2)}) async-start(bf16[32,8,1024]{2,1,0:T(8,128)(2,1)} %fusion.37), calls=%async_computation.2 | async-start | bytes 1048576 | tf_op jit(solution)/shard_map/all_to_all | solution.py:74
  117.7 5.6 %copy-start.16 = (bf16[1,1024,2048]{2,1,0:T(8,128)(2,1)S(1)}, bf16[1,1024,2048]{2,1,0:T(8,128)(2,1)}, u32[]{:S(2)}) copy-start(bf16[1,1024,2048]{2,1,0:T(8,128)(2,1)} %param.10) | copy-start | bytes 12582916
  122.3 1.0 copy-start.10
  134.5 22.8 %all-to-all-start.5 = ((bf16[32,8,1024]{2,1,0:T(8,128)(2,1)}), bf16[32,8,1024]{2,1,0:T(8,128)(2,1)}, u32[]{:S(2)}, u32[]{:S(2)}) async-start(bf16[32,8,1024]{2,1,0:T(8,128)(2,1)} %fusion.34), calls=%async_computation.5 | async-start | bytes 1048576 | tf_op jit(solution)/shard_map/all_to_all | solution.py:74
  140.5 332.3 %all-reduce.3.cloned.1.call-start = ((), (), s32[]{:S(2)}) async-start(), calls=%async_computation.10 | async-start | bytes 8388608
  157.3 2.2 copy-start.5
  157.3 2.2 copy-start.7
  159.5 1.0 copy-start.12
  163.5 311.4 %reduce-scatter.6.cloned.1.call-start = ((), (), s32[]{:S(2)}) async-start(), calls=%async_computation.9 | async-start | bytes 4718592 | tf_op jit(solution)/shard_map/reduce_scatter | solution.py:102
  163.5 3.3 copy-start.8
  171.3 1.1 copy-start.4
  171.3 303.6 %reduce-scatter.4.cloned.1.call-start = ((), (), s32[]{:S(2)}) async-start(), calls=%async_computation.8 | async-start | bytes 4718592 | tf_op jit(solution)/shard_map/reduce_scatter | solution.py:99
  172.3 2.6 copy-start.11
Sparse Core Ops, SparseCore 0:
  163.6 309.2 all-reduce.2
Sparse Core Ops, SparseCore 1:
  171.4 53.8 reduce-scatter.5
  228.2 58.8 reduce-scatter.3
where the time goes:
time: 484 us; the launch traced here: 482 us
  waiting for transfers between devices  366 us (76%)
  matrix products  52.9 us (11%)
  starting transfers between devices  40 us (8%)
  between operations  15.8 us (3%)
  local copies, waits for them, and re-layouts  7.07 us (1%)
    unnamed x4, waiting for transfers between devices  295 us
    all_to_all x2, waiting for transfers between devices, body(): lax.all_to_all(send_norm.reshape(experts, capacity, model_width), 'expert...  31.1 us
    all_to_all x2, waiting for transfers between devices, body(): lax.all_to_all(back_rows.reshape(experts, capacity, model_width), 'expert...  23.7 us
    all_to_all x2, starting transfers between devices, body(): lax.all_to_all(send_norm.reshape(experts, capacity, model_width), 'expert...  16.8 us
    all_to_all x2, waiting for transfers between devices, body(): lax.all_to_all(send_grad.reshape(experts, capacity, model_width), 'expert...  16.4 us
    all_to_all x2, starting transfers between devices, body(): lax.all_to_all(back_rows.reshape(experts, capacity, model_width), 'expert...  11.9 us
    all_to_all x2, starting transfers between devices, body(): lax.all_to_all(send_grad.reshape(experts, capacity, model_width), 'expert...  11.1 us
  transfers between devices with their start and end apart: 9, of which 7 were waited for; matrix products, arithmetic and copies ran while one was open for 9% of the time, Pallas kernels for 0%

commit v1 on v0

v1 whole, which is shorter than its diff:
```python
import jax
import jax.numpy as jnp
from jax import lax
from jax.sharding import PartitionSpec as P

epsilon = 1e-06
contract_rows = (((0,), (0,)), ((), ()))


def silu_pair(pre_value):
    gate_value = jax.nn.sigmoid(pre_value)
    return (pre_value * gate_value, gate_value * (1.0 + pre_value * (1.0 - gate_value)))


def body(cell_rows, cotangent, cluster_ids, enc_weight, up_weight, down_weight):
    experts = lax.axis_size("expert")
    dp_count = lax.axis_size("dp")
    batch_count, local_rows, width = cell_rows.shape
    capacity = 8
    w_up = up_weight[0]
    w_down = down_weight[0]
    rows = batch_count * local_rows
    slots = experts * batch_count * capacity
    features = cell_rows.reshape(rows, width)
    pre_enc = jnp.dot(features, enc_weight, preferred_element_type=jnp.float32)
    silu_enc, slope_enc = silu_pair(pre_enc)
    encoded = features.astype(jnp.float32) + silu_enc
    inverse = lax.rsqrt(jnp.mean(encoded * encoded, axis=1, keepdims=True) + epsilon)
    normed = (encoded * inverse).astype(jnp.bfloat16)
    labels = cluster_ids[:, :, 0]
    onehot = (labels[:, :, None] == jnp.arange(experts, dtype=jnp.int32)).astype(jnp.int32)
    rank = jnp.sum((jnp.cumsum(onehot, axis=1) - onehot) * onehot, axis=2)
    batch_of = jnp.arange(batch_count, dtype=jnp.int32)[:, None]
    target = ((labels * batch_count + batch_of) * capacity + rank).reshape(rows)
    placer = (jnp.arange(slots, dtype=jnp.int32)[:, None] == target[None, :]).astype(jnp.bfloat16)
    both = jnp.concatenate([normed, cotangent.reshape(rows, width)], axis=1)
    send = jnp.dot(placer, both, preferred_element_type=jnp.float32).astype(jnp.bfloat16)
    recv = lax.all_to_all(
        send.reshape(experts, batch_count * capacity, 2 * width), "expert", split_axis=0, concat_axis=0, tiled=True
    ).reshape(slots, 2 * width)
    norm_rows, grad_rows = recv[:, :width], recv[:, width:]
    pre_exp = jnp.dot(norm_rows, w_up, preferred_element_type=jnp.float32)
    silu_exp, slope_exp = silu_pair(pre_exp)
    active = silu_exp.astype(jnp.bfloat16)
    act_grad = jnp.dot(grad_rows, w_down, preferred_element_type=jnp.float32)
    pre_grad = (act_grad * slope_exp).astype(jnp.bfloat16)
    up_part = lax.dot_general(norm_rows, pre_grad, contract_rows, preferred_element_type=jnp.float32).astype(jnp.bfloat16)
    down_part = lax.dot_general(grad_rows, active, contract_rows, preferred_element_type=jnp.float32).astype(jnp.bfloat16)
    up_sum = lax.psum_scatter(up_part, "dp", scatter_dimension=0, tiled=True)
    down_sum = lax.psum_scatter(down_part, "dp", scatter_dimension=0, tiled=True)
    back_rows = lax.dot_general(
        pre_grad, w_up, (((1,), (1,)), ((), ())), preferred_element_type=jnp.float32
    ).astype(jnp.bfloat16)
    returned = lax.all_to_all(
        back_rows.reshape(experts, batch_count * capacity, width), "expert", split_axis=0, concat_axis=0, tiled=True
    ).reshape(slots, width)
    norm_grad = lax.dot_general(placer, returned, contract_rows, preferred_element_type=jnp.float32)
    enc_rows_grad = inverse * norm_grad - inverse * inverse * inverse * encoded * jnp.mean(
        norm_grad * encoded, axis=1, keepdims=True
    )
    enc_pre_grad = (enc_rows_grad * slope_enc).astype(jnp.bfloat16)
    enc_part = lax.dot_general(features, enc_pre_grad, contract_rows, preferred_element_type=jnp.float32)
    enc_dp = lax.psum_scatter(enc_part, "dp", scatter_dimension=0, tiled=True)
    enc_sum = lax.psum_scatter(enc_dp, "expert", scatter_dimension=0, tiled=True)
    return (enc_sum, up_sum[None], down_sum[None])


def solution(mesh):
    in_specs = (
        P(None, ("dp", "expert"), None),
        P(None, ("dp", "expert"), None),
        P(None, ("dp", "expert"), None),
        P(),
        P("expert", None, None),
        P("expert", None, None),
    )
    out_specs = (P(("dp", "expert"), None), P("expert", "dp", None), P("expert", "dp", None))
    return jax.shard_map(body, mesh=mesh, in_specs=in_specs, out_specs=out_specs, check_vma=False)
```

time: 484 us -> 587 us (1.21)
  blocking collectives: 0 us -> 97.6 us
  waiting for transfers between devices: 366 us -> 440 us
  starting transfers between devices: 40 us -> 0.34 us
  matrix products: 52.9 us -> 27.6 us
    reduce_scatter x2 -> x3, waiting for transfers between devices: 0.01 us -> 166 us  [the longest x1 57.5 us: body(): up_sum = lax.psum_scatter(up_part, 'dp', scatter_dimension=0, tiled=True)]
    all_to_all x0 -> x2, blocking collectives: none -> 97.6 us  [the longest x1 62.5 us: body(): lax.all_to_all(send.reshape(experts, batch_count * capacity, 2 * width),...]
    all_to_all x6 -> x0, waiting for transfers between devices: 71.2 us -> none  [the longest x2 31.1 us: body(): lax.all_to_all(send_norm.reshape(experts, capacity, model_width), 'expert...]
    all_to_all x6 -> x0, starting transfers between devices: 39.9 us -> none  [the longest x2 16.8 us: body(): lax.all_to_all(send_norm.reshape(experts, capacity, model_width), 'expert...]
    unnamed x4 -> x5, waiting for transfers between devices: 295 us -> 274 us
    dot_general x6 -> x2, matrix products: 11.8 us -> 1.29 us  [the longest x1 0.71 us: body(): jnp.dot(placer, both, preferred_element_type=jnp.float32)]
    dot_general x2 -> x1, matrix products: 9.13 us -> 3.01 us  [body(): act_grad = jnp.dot(grad_rows, w_down, preferred_element_type=jnp.float32)]
  transfers between devices with their start and end apart: 9 -> 4, of which waited for: 7 -> 4; matrix products, arithmetic and copies ran while one was open for 9% -> 3% of each run, Pallas kernels for 0% -> 0%
where the time goes in v1:
time: 587 us
  waiting for transfers between devices  440 us (75%)
  blocking collectives  97.6 us (17%)
  matrix products  27.6 us (5%)
  between operations  14.6 us (2%)
    unnamed x5, waiting for transfers between devices  274 us
    all_to_all x1, blocking collectives, body(): lax.all_to_all(send.reshape(experts, batch_count * capacity, 2 * width),...  62.5 us
    reduce_scatter x1, waiting for transfers between devices, body(): up_sum = lax.psum_scatter(up_part, 'dp', scatter_dimension=0, tiled=True)  57.5 us
    reduce_scatter x1, waiting for transfers between devices, body(): lax.psum_scatter(down_part, 'dp', scatter_dimension=0, tiled=True)  55.9 us
    reduce_scatter x1, waiting for transfers between devices, body(): enc_dp = lax.psum_scatter(enc_part, 'dp', scatter_dimension=0, tiled=True)  52.7 us
    all_to_all x1, blocking collectives, body(): lax.all_to_all(back_rows.reshape(experts, batch_count * capacity, width),...  35.1 us
  transfers between devices with their start and end apart: 4, of which 4 were waited for; matrix products, arithmetic and copies ran while one was open for 3% of the time, Pallas kernels for 0%

profile of v1, /device:TPU:1, one launch (start us, length us, event | category | flops | bytes accessed | tf_op | source)
XLA Modules:
  0.0 586.8 jit_solution(9130571218406253434)
XLA Ops:
  7.2 0.0 copy-start
  7.2 0.0 reduce-scatter.5.cloned.1.call-start
  7.2 0.8 broadcast_multiply_fusion
  8.0 0.8 fusion.26
  8.8 0.2 reduce_window_sum.11
  9.0 0.9 select_reduce_fusion
  9.9 0.0 copy-done
  9.9 0.0 copy-start.2
  9.9 2.3 multiply_reduce_fusion.1
  12.2 0.1 multiply_convert_fusion.4
  12.3 0.0 copy-done.2
  12.3 0.0 copy-start.4
  12.3 0.7 convolution_convert_fusion.2
  13.1 62.5 %all_to_all.10 = bf16[32,16,2048]{2,1,0:T(8,128)(2,1)S(1)} all-to-all(bf16[32,16,2048]{2,1,0:T(8,128)(2,1)S(1)} %bitcast.43), channel_id=1, replica_groups=mesh['dp'=8,'expert'=32] {'expert'}, dimensions={0} | all-to-all | bytes 4194304 | tf_op jit(solution)/shard_map/all_to_all | solution.py:38
  75.5 0.0 copy-start.1
  75.5 0.0 copy-done.4
  75.5 0.0 copy-start.3
  75.5 2.4 fusion.2
  77.9 0.0 copy-done.1
  77.9 0.6 copy-done.3
  78.5 0.0 copy-start.8
  78.5 3.0 multiply_convert_fusion.1
  81.5 0.0 copy-done.8
  81.5 0.0 copy-start.7
  81.5 2.4 fusion.9
  83.9 0.0 copy-done.7
  83.9 0.0 copy-start.5
  83.9 35.1 %all_to_all.11 = bf16[32,16,1024]{2,1,0:T(8,128)(2,1)S(1)} all-to-all(bf16[32,16,1024]{2,1,0:T(8,128)(2,1)S(1)} %bitcast.49), channel_id=1, replica_groups=mesh['dp'=8,'expert'=32] {'expert'}, dimensions={0} | all-to-all | bytes 2097152 | tf_op jit(solution)/shard_map/all_to_all | solution.py:54
  119.1 0.6 multiply_reduce_fusion
  119.7 0.0 copy-done.5
  119.7 3.1 convolution_bitcast_fusion
  122.7 0.0 reduce-scatter.5.cloned.1.call-update
  122.8 0.0 all-reduce.3.cloned.1.call-start
  122.8 52.7 %reduce-scatter.5.cloned.1.call-done = f32[128,1024]{0,1:T(8,128)} async-done(((f32[1024,1024]{0,1:T(8,128)}), f32[128,1024]{0,1:T(8,128)}) %reduce-scatter.5.cloned.1.call-update) | async-done | bytes 524304 | tf_op jit(solution)/shard_map/reduce_scatter | solution.py:63
  175.5 0.0 all-reduce.3.cloned.1.call-update
  175.6 0.2 reduce-scatter.9.cloned.1.call-start
  175.8 7.0 %convolution_convert_fusion = bf16[1024,2048]{1,0:T(8,128)(2,1)} fusion(f32[512,2048]{1,0:T(8,128)} %copy-done.8, bf16[512,2048]{1,0:T(8,128)(2,1)} %bitcast.47), kind=kOutput, calls=%fused_computation.9 | convolution fusion | flops 2154823680 | bytes 9437184 | tf_op jit(solution)/shard_map/dot_general | solution.py:48
  182.8 0.0 reduce-scatter.9.cloned.1.call-update
  182.8 0.0 reduce-scatter.7.cloned.1.call-start
  182.8 6.2 %convolution_convert_fusion.1 = bf16[1024,2048]{1,0:T(8,128)(2,1)} fusion(bf16[512,2048]{1,0:T(8,128)(2,1)} %copy-done.7, bf16[512,2048]{1,0:T(8,128)(2,1)} %bitcast.48), kind=kOutput, calls=%fused_computation.10 | convolution fusion | flops 2149580800 | bytes 7340032 | tf_op jit(solution)/shard_map/dot_general | solution.py:47
  189.1 0.0 copy-start.6
  189.1 0.0 reduce-scatter.7.cloned.1.call-update
  189.1 0.6 copy-done.6
  189.8 0.6 dynamic-slice
  191.0 273.8 %all-reduce.3.cloned.1.call-done = f32[128,1024]{0,1:T(8,128)} async-done(((f32[128,1024]{0,1:T(8,128)}), f32[128,1024]{0,1:T(8,128)}) %all-reduce.3.cloned.1.call-update) | async-done | bytes 524304
  464.8 1.2 constant_dynamic-slice_fusion
  466.0 0.8 copy.10
  466.8 55.9 %reduce-scatter.9.cloned.1.call-done = bf16[128,2048]{1,0:T(8,128)(2,1)} async-done(((bf16[1024,2048]{1,0:T(8,128)(2,1)}), bf16[128,2048]{1,0:T(8,128)(2,1)}) %reduce-scatter.9.cloned.1.call-update) | async-done | bytes 524304 | tf_op jit(solution)/shard_map/reduce_scatter | solution.py:50
  522.7 57.5 %reduce-scatter.7.cloned.1.call-done = bf16[128,2048]{1,0:T(8,128)(2,1)} async-done(((bf16[1024,2048]{1,0:T(8,128)(2,1)}), bf16[128,2048]{1,0:T(8,128)(2,1)}) %reduce-scatter.7.cloned.1.call-update) | async-done | bytes 524304 | tf_op jit(solution)/shard_map/reduce_scatter | solution.py:49
  (3 shorter events, 0.0 us)
Async XLA Ops:
  7.2 2.7 copy-start
  7.2 168.4 %reduce-scatter.5.cloned.1.call-start = ((), (), s32[]{:S(2)}) async-start(), calls=%async_computation.5 | async-start | bytes 4718592 | tf_op jit(solution)/shard_map/reduce_scatter | solution.py:63
  9.9 2.4 copy-start.2
  12.3 63.2 %copy-start.4 = (bf16[1,1024,2048]{2,1,0:T(8,128)(2,1)S(1)}, bf16[1,1024,2048]{2,1,0:T(8,128)(2,1)}, u32[]{:S(2)}) copy-start(bf16[1,1024,2048]{2,1,0:T(8,128)(2,1)} %param.10) | copy-start | bytes 12582916
  75.5 2.4 copy-start.1
  75.5 2.9 copy-start.3
  78.5 3.0 copy-start.8
  81.5 2.4 copy-start.7
  83.9 35.7 %copy-start.5 = (bf16[2,128,1024]{2,1,0:T(8,128)(2,1)S(1)}, bf16[2,128,1024]{2,1,0:T(8,128)(2,1)}, u32[]{:S(2)}) copy-start(bf16[2,128,1024]{2,1,0:T(8,128)(2,1)} %param.6) | copy-start | bytes 1572868
  122.8 342.0 %all-reduce.3.cloned.1.call-start = ((), (), s32[]{:S(2)}) async-start(), calls=%async_computation.8 | async-start | bytes 1048576
  175.6 347.2 %reduce-scatter.9.cloned.1.call-start = ((), (), s32[]{:S(2)}) async-start(), calls=%async_computation.7 | async-start | bytes 4718592 | tf_op jit(solution)/shard_map/reduce_scatter | solution.py:50
  182.8 397.5 %reduce-scatter.7.cloned.1.call-start = ((), (), s32[]{:S(2)}) async-start(), calls=%async_computation.6 | async-start | bytes 4718592 | tf_op jit(solution)/shard_map/reduce_scatter | solution.py:49
  189.1 0.7 copy-start.6
Sparse Core Ops, SparseCore 0:
  122.9 52.6 reduce-scatter.4
  178.2 286.5 all-reduce.2
  467.9 54.7 reduce-scatter.8
  525.7 54.5 reduce-scatter.6

commit v2 on v1

v2 whole, which is shorter than its diff:
```python
import jax
import jax.numpy as jnp
from jax import lax
from jax.experimental import pallas as pl
from jax.experimental.pallas import tpu as pltpu
from jax.sharding import PartitionSpec as P

MESH = pl.DeviceIdType.MESH
F32 = jnp.float32
BF16 = jnp.bfloat16
epsilon = 1e-06

N_DP = 8
N_EX = 32
D = 1024
H = 2048
ROWS = 128
MICRO = 2
ALL_ROWS = MICRO * ROWS
CAP = 8
SLOT = MICRO * CAP
SLOTS = N_EX * SLOT
WIDE = 512


def dot(a, b):
    return jnp.dot(a, b, preferred_element_type=F32)


def dot_nt(a, b):
    return lax.dot_general(a, b, (((1,), (1,)), ((), ())), preferred_element_type=F32)


def dot_tn(a, b):
    return lax.dot_general(a, b, (((0,), (0,)), ((), ())), preferred_element_type=F32)


def aligned(index, size):
    return pl.ds(pl.multiple_of(index * size, size), size)


def loop(low, high, step):
    def body(index, carry):
        step(index)
        return carry

    lax.fori_loop(low, high, body, 0)


def kernel(
    cell, cot, ids, encw, up_hbm, down_hbm,
    enc_out, up_out, down_out,
    w_up, w_down, both, send, recv, pre_grad, active, back, ret,
    enc_s, slope_s, inv_s, placer, fperm, egrad,
    part, rs_recv, z_recv,
    e_own, e_send, e_recv, x_own, x_send, x_recv, h_own, h_send, h_recv, d_send, d_recv,
    w_sem, disp_s, disp_r, ret_s, ret_r, rs_s, rs_r, z_s, z_r, c_s, c_r, x_s, x_r, h_s, h_r, d_s, d_r,
):
    d = lax.axis_index("dp")
    e = lax.axis_index("expert")
    z_lo, y = d // 4, d % 4
    z_hi, plane = e // 8, e % 8
    x, core = plane // 2, plane % 2
    right = (z_lo * 4 + (y + 1) % 4, e)
    left = (z_lo * 4 + (y + 3) % 4, e)
    mate = ((1 - z_lo) * 4 + y, e)

    def copy(src, dst, s, r, who):
        return pltpu.make_async_remote_copy(
            src_ref=src, dst_ref=dst, send_sem=s, recv_sem=r, device_id=who, device_id_type=MESH
        )

    w_copies = [
        pltpu.make_async_copy(up_hbm.at[0], w_up, w_sem.at[0]),
        pltpu.make_async_copy(down_hbm.at[0], w_down, w_sem.at[1]),
    ]
    for item in w_copies:
        item.start()

    barrier = pltpu.get_barrier_semaphore()

    def greet_expert(k):
        pl.semaphore_signal(barrier, inc=1, device_id=(d, (e + k) % N_EX), device_id_type=MESH)

    def greet_dp(k):
        pl.semaphore_signal(barrier, inc=1, device_id=((d + k) % N_DP, e), device_id_type=MESH)

    loop(1, N_EX, greet_expert)
    loop(1, N_DP, greet_dp)

    lower = (
        lax.broadcasted_iota(jnp.int32, (ROWS, ROWS), 1) < lax.broadcasted_iota(jnp.int32, (ROWS, ROWS), 0)
    ).astype(BF16)
    for m in range(MICRO):
        label = ids[m]
        onehot = (label == lax.broadcasted_iota(jnp.int32, (ROWS, 128), 1)).astype(F32)
        before = dot(lower, onehot.astype(BF16))
        rank = jnp.sum(before * onehot, axis=1, keepdims=True).astype(jnp.int32)
        target = label * SLOT + m * CAP + rank
        slots = lax.broadcasted_iota(jnp.int32, (ROWS, SLOTS), 1)
        placer[m * ROWS : (m + 1) * ROWS, :] = (slots == target).astype(F32).astype(BF16)

    def encode(i):
        m, part_row = i // 2, i % 2
        rows = aligned(part_row, 64)
        feat = cell[m, rows, :]
        pre = dot(feat, encw[...])
        gate = jax.nn.sigmoid(pre)
        encoded = feat.astype(F32) + pre * gate
        inverse = lax.rsqrt(jnp.sum(encoded * encoded, axis=1, keepdims=True) * (1.0 / D) + epsilon)
        out = aligned(i, 64)
        enc_s[out, :] = encoded
        slope_s[out, :] = gate * (1.0 + pre * (1.0 - gate))
        inv_s[out, :] = jnp.broadcast_to(inverse, (64, 128))
        both[out, :D] = (encoded * inverse).astype(BF16)
        both[out, D:] = cot[m, rows, :]

    loop(0, 4, encode)
    pl.semaphore_wait(barrier, N_EX + N_DP - 2)

    def dispatch(c):
        return copy(send.at[aligned(c, SLOT), :], recv.at[aligned(e, SLOT), :], disp_s.at[c], disp_r.at[e], (d, c))

    def arrival(c):
        return copy(send.at[aligned(c, SLOT), :], recv.at[aligned(c, SLOT), :], disp_s.at[c], disp_r.at[c], (d, c))

    order = (0, 1, 3, 2)

    def peer(hop, k):
        return ((z_hi + hop) % 4) * 8 + (plane + k) % 8

    for hop in order:
        h = (z_hi + hop) % 4
        picks = placer[:, aligned(h, 128)]
        send[aligned(h, 128), :] = dot_tn(picks, both[...]).astype(BF16)
        loop(1 if hop == 0 else 0, 8, lambda k: dispatch(peer(hop, k)).start())
    recv[aligned(e, SLOT), :] = send[aligned(e, SLOT), :]

    def permute(n):
        col = lax.broadcasted_iota(jnp.int32, (1, 256), 1) + n * 256
        nat = (
            (col & 3)
            + (((col >> 2) & 7) << 7)
            + (((col >> 5) & 3) << 5)
            + (((col >> 7) & 3) << 3)
            + ((col >> 9) << 2)
        )
        pick = (lax.broadcasted_iota(jnp.int32, (D, 256), 0) == nat).astype(F32).astype(BF16)
        for m in range(MICRO):
            fperm[m * ROWS : (m + 1) * ROWS, aligned(n, 256)] = dot(cell[m], pick).astype(BF16)

    loop(0, 4, permute)
    for item in w_copies:
        item.wait()

    def give_back(c):
        return copy(back.at[aligned(c, SLOT), :], ret.at[aligned(e, SLOT), :], ret_s.at[c], ret_r.at[e], (d, c))

    def came_back(c):
        return copy(back.at[aligned(c, SLOT), :], ret.at[aligned(c, SLOT), :], ret_s.at[c], ret_r.at[c], (d, c))

    for hop in order:
        h = (z_hi + hop) % 4
        group = aligned(h, 128)
        loop(1 if hop == 0 else 0, 8, lambda k: arrival(peer(hop, k)).wait_recv())

        def hidden(n):
            cols = aligned(n, WIDE)
            pre = dot(recv[group, :D], w_up[:, cols])
            act_grad = dot(recv[group, D:], w_down[:, cols])
            gate = jax.nn.sigmoid(pre)
            active[group, cols] = (pre * gate).astype(BF16)
            pre_grad[group, cols] = (act_grad * (gate * (1.0 + pre * (1.0 - gate)))).astype(BF16)

        loop(0, H // WIDE, hidden)

        def backward(n):
            back[group, aligned(n, 256)] = dot_nt(pre_grad[group, :], w_up[aligned(n, 256), :]).astype(BF16)

        loop(0, D // 256, backward)
        if hop == 0:
            loop(1, 8, lambda k: give_back(peer(0, k)).start())
    for hop in order[1:]:
        loop(0, 8, lambda k: give_back(peer(hop, k)).start())
    ret[aligned(e, SLOT), :] = back[aligned(e, SLOT), :]

    def grads(p, q, block):
        up_t = recv[:, aligned(block, 128)].T
        down_t = recv[:, aligned(block + D // 128, 128)].T

        def piece(n):
            cols = aligned(n, WIDE)
            part[p, q, 0, :, cols] = dot(up_t, pre_grad[:, cols]).astype(BF16)
            part[p, q, 1, :, cols] = dot(down_t, active[:, cols]).astype(BF16)

        loop(0, H // WIDE, piece)

    def rs(p, slot):
        q, which, who = ((0, 0, right), (0, 1, left), (1, 1, right), (2, 0, left), (1, 0, right), (2, 1, left))[slot]
        return copy(part.at[p, q, which], rs_recv.at[p, slot], rs_s.at[p, slot], rs_r.at[p, slot], who)

    def add_into(p, q, which, others):
        def piece(n):
            rows = aligned(n, 32)
            total = part[p, q, which, rows, :].astype(F32)
            for slot in others:
                total = total + rs_recv[p, slot, rows, :].astype(F32)
            part[p, q, which, rows, :] = total.astype(BF16)

        loop(0, 4, piece)

    for p in range(2):
        base = ((1 - z_lo) if p == 0 else z_lo) * 4
        grads(p, 0, base + (y + 2) % 4)
        rs(p, 0).start()
        rs(p, 1).start()
        if p == 0:
            grads(p, 1, base + (y + 1) % 4)
            rs(p, 2).start()
            grads(p, 2, base + (y + 3) % 4)
            rs(p, 3).start()
            grads(p, 3, base + y)

    def combine(p):
        rs(p, 0).wait_recv()
        add_into(p, 1, 0, (0,))
        rs(p, 4).start()
        rs(p, 1).wait_recv()
        add_into(p, 2, 1, (1,))
        rs(p, 5).start()

    combine(0)
    base = z_lo * 4
    grads(1, 1, base + (y + 1) % 4)
    rs(1, 2).start()
    grads(1, 2, base + (y + 3) % 4)
    rs(1, 3).start()
    grads(1, 3, base + y)

    loop(1, 8, lambda k: came_back(peer(0, k)).wait_recv())
    for hop in order[1:]:
        loop(0, 8, lambda k: came_back(peer(hop, k)).wait_recv())

    def encoder_back(i):
        rows = aligned(i, 64)
        norm_grad = dot(placer[rows, :], ret[...])
        encoded = enc_s[rows, :]
        inverse = inv_s[rows, 0:1]
        mean = jnp.sum(norm_grad * encoded, axis=1, keepdims=True) * (1.0 / D)
        grad = inverse * norm_grad - inverse * inverse * inverse * encoded * mean
        egrad[rows, :] = (grad * slope_s[rows, :]).astype(BF16)

    loop(0, 4, encoder_back)

    def enc_piece(index):
        return dot(fperm[:, aligned(index, 128)].T, egrad[...])

    def enc_other(n):
        e_send[aligned(n, 128), :] = enc_piece((1 - core) * 4 + n).astype(BF16)

    def enc_own(n):
        e_own[aligned(n, 128), :] = enc_piece(core * 4 + n)

    loop(0, 4, enc_other)
    to_core = copy(e_send, e_recv, c_s.at[0], c_r.at[0], (d, e + 1 - 2 * core))
    to_core.start()
    loop(0, 4, enc_own)

    combine(1)

    to_core.wait_recv()

    def x_device(k):
        return (x + k) % 4

    def x_copy(k):
        to = x_device(k)
        return copy(x_send.at[to], x_recv.at[x], x_s.at[to], x_r.at[x], (d, (z_hi * 4 + to) * 2 + core))

    def x_from(k):
        to = x_device(k)
        return copy(x_send.at[to], x_recv.at[to], x_s.at[to], x_r.at[to], (d, (z_hi * 4 + to) * 2 + core))

    for k in (2, 1, 3):
        rows = aligned(x_device(k), 128)
        x_send[x_device(k)] = (e_own[rows, :] + e_recv[rows, :].astype(F32)).astype(BF16)
        x_copy(k).start()
    rows = aligned(x, 128)
    x_own[...] = e_own[rows, :] + e_recv[rows, :].astype(F32)

    def finish(p):
        rs(p, 3).wait_recv()
        rs(p, 4).wait_recv()
        rs(p, 2).wait_recv()
        rs(p, 5).wait_recv()

    finish(0)
    to_mate = [copy(part.at[0, 3, w], z_recv.at[w], z_s.at[w], z_r.at[w], mate) for w in range(2)]
    add_into(0, 3, 0, (3, 4))
    to_mate[0].start()
    add_into(0, 3, 1, (2, 5))
    to_mate[1].start()

    for k in (1, 3, 2):
        x_from(k).wait_recv()

    def h_copy(k):
        to = (z_hi + k) % 4
        return copy(h_send.at[to], h_recv.at[z_hi], h_s.at[to], h_r.at[z_hi], (d, to * 8 + plane))

    def h_from(k):
        to = (z_hi + k) % 4
        return copy(h_send.at[to], h_recv.at[to], h_s.at[to], h_r.at[to], (d, to * 8 + plane))

    def x_sum(to):
        rows = aligned(to, 32)
        total = x_own[rows, :]
        for k in (1, 2, 3):
            total = total + x_recv[x_device(k), rows, :].astype(F32)
        return total

    for k in (2, 1, 3):
        h_send[(z_hi + k) % 4] = x_sum((z_hi + k) % 4).astype(BF16)
        h_copy(k).start()
    h_own[...] = x_sum(z_hi)
    for k in (1, 3, 2):
        h_from(k).wait_recv()
    total = h_own[...]
    for k in (1, 2, 3):
        total = total + h_recv[(z_hi + k) % 4].astype(F32)
    d_send[...] = total.reshape(N_DP, 4, D)

    def d_copy(k):
        to = (d + k) % N_DP
        return copy(d_send.at[to], d_recv.at[d], d_s.at[to], d_r.at[d], (to, e))

    def d_from(k):
        to = (d + k) % N_DP
        return copy(d_send.at[to], d_recv.at[to], d_s.at[to], d_r.at[to], (to, e))

    loop(1, N_DP, lambda k: d_copy(k).start())

    finish(1)
    for w, (out, others) in enumerate(((up_out, (3, 4)), (down_out, (2, 5)))):
        to_mate[w].wait_recv()

        def piece(n):
            rows = aligned(n, 32)
            total = part[1, 3, w, rows, :].astype(F32) + z_recv[w, rows, :].astype(F32)
            for slot in others:
                total = total + rs_recv[1, slot, rows, :].astype(F32)
            out[0, rows, :] = total.astype(BF16)

        loop(0, 4, piece)

    loop(1, N_DP, lambda k: d_from(k).wait_recv())
    total = d_send[d]
    for k in range(1, N_DP):
        total = total + d_recv[(d + k) % N_DP]
    enc_out[...] = total

    for hop in order:
        loop(1 if hop == 0 else 0, 8, lambda k: dispatch(peer(hop, k)).wait_send())
        loop(1 if hop == 0 else 0, 8, lambda k: give_back(peer(hop, k)).wait_send())
    for p in range(2):
        for slot in range(6):
            rs(p, slot).wait_send()
    for w in range(2):
        to_mate[w].wait_send()
    to_core.wait_send()
    for k in (1, 2, 3):
        x_copy(k).wait_send()
        h_copy(k).wait_send()
    loop(1, N_DP, lambda k: d_copy(k).wait_send())


def body(cell_rows, cotangent, cluster_ids, enc_weight, up_weight, down_weight):
    vmem = pl.BlockSpec(memory_space=pltpu.VMEM)
    hbm = pl.BlockSpec(memory_space=pl.ANY)
    dma = pltpu.SemaphoreType.DMA
    return pl.pallas_call(
        kernel,
        name="step",
        out_shape=(
            jax.ShapeDtypeStruct((4, D), F32),
            jax.ShapeDtypeStruct((1, 128, H), BF16),
            jax.ShapeDtypeStruct((1, 128, H), BF16),
        ),
        in_specs=[vmem, vmem, vmem, vmem, hbm, hbm],
        out_specs=(vmem, vmem, vmem),
        scratch_shapes=[
            pltpu.VMEM((D, H), BF16),
            pltpu.VMEM((D, H), BF16),
            pltpu.VMEM((ALL_ROWS, 2 * D), BF16),
            pltpu.VMEM((SLOTS, 2 * D), BF16),
            pltpu.VMEM((SLOTS, 2 * D), BF16),
            pltpu.VMEM((SLOTS, H), BF16),
            pltpu.VMEM((SLOTS, H), BF16),
            pltpu.VMEM((SLOTS, D), BF16),
            pltpu.VMEM((SLOTS, D), BF16),
            pltpu.VMEM((ALL_ROWS, D), F32),
            pltpu.VMEM((ALL_ROWS, D), F32),
            pltpu.VMEM((ALL_ROWS, 128), F32),
            pltpu.VMEM((ALL_ROWS, SLOTS), BF16),
            pltpu.VMEM((ALL_ROWS, D), BF16),
            pltpu.VMEM((ALL_ROWS, D), BF16),
            pltpu.VMEM((2, 4, 2, 128, H), BF16),
            pltpu.VMEM((2, 6, 128, H), BF16),
            pltpu.VMEM((2, 128, H), BF16),
            pltpu.VMEM((512, D), F32),
            pltpu.VMEM((512, D), BF16),
            pltpu.VMEM((512, D), BF16),
            pltpu.VMEM((128, D), F32),
            pltpu.VMEM((4, 128, D), BF16),
            pltpu.VMEM((4, 128, D), BF16),
            pltpu.VMEM((32, D), F32),
            pltpu.VMEM((4, 32, D), BF16),
            pltpu.VMEM((4, 32, D), BF16),
            pltpu.VMEM((N_DP, 4, D), F32),
            pltpu.VMEM((N_DP, 4, D), F32),
            dma((2,)),
            dma((N_EX,)),
            dma((N_EX,)),
            dma((N_EX,)),
            dma((N_EX,)),
            dma((2, 6)),
            dma((2, 6)),
            dma((2,)),
            dma((2,)),
            dma((1,)),
            dma((1,)),
            dma((4,)),
            dma((4,)),
            dma((4,)),
            dma((4,)),
            dma((N_DP,)),
            dma((N_DP,)),
        ],
        compiler_params=pltpu.CompilerParams(
            collective_id=0, has_side_effects=True, vmem_limit_bytes=62 << 20
        ),
    )(cell_rows, cotangent, cluster_ids, enc_weight, up_weight, down_weight)


def solution(mesh):
    in_specs = (
        P(None, ("dp", "expert"), None),
        P(None, ("dp", "expert"), None),
        P(None, ("dp", "expert"), None),
        P(),
        P("expert", None, None),
        P("expert", None, None),
    )
    out_specs = (P(("dp", "expert"), None), P("expert", "dp", None), P("expert", "dp", None))
    return jax.shard_map(body, mesh=mesh, in_specs=in_specs, out_specs=out_specs, check_vma=False)
```

time: 587 us -> 162 us (0.28)
  waiting for transfers between devices: 440 us -> 0 us
  Pallas kernels: 0 us -> 153 us
  blocking collectives: 97.6 us -> 0 us
  matrix products: 27.6 us -> 0 us
  between operations: 14.6 us -> 0.64 us
    unnamed x5 -> x0, waiting for transfers between devices: 274 us -> none
    reduce_scatter x3 -> x0, waiting for transfers between devices: 166 us -> none  [the longest x1 57.5 us: body(): up_sum = lax.psum_scatter(up_part, 'dp', scatter_dimension=0, tiled=True)]
    pallas_call x0 -> x1, Pallas kernels: none -> 153 us  [body(): pl.pallas_call(kernel, name='step', out_shape=(jax.ShapeDtypeStruct((4, D...]
    all_to_all x2 -> x0, blocking collectives: 97.6 us -> none  [the longest x1 62.5 us: body(): lax.all_to_all(send.reshape(experts, batch_count * capacity, 2 * width),...]
    dot_general x9 -> x0, matrix products: 27.6 us -> none  [the longest x1 6.96 us: body(): lax.dot_general(grad_rows, active, contract_rows, preferred_element_type=...]
  transfers between devices with their start and end apart: 4 -> 0, of which waited for: 4 -> 0; matrix products, arithmetic and copies ran while one was open for 3% -> 0% of each run, Pallas kernels for 0% -> 0%
where the time goes in v2:
time: 162 us; the launch traced here: 160 us
  Pallas kernels  153 us (94%)
  local copies, waits for them, and re-layouts  6.56 us (4%)
    pallas_call x1, Pallas kernels, body(): pl.pallas_call(kernel, name='step', out_shape=(jax.ShapeDtypeStruct((4, D...  153 us
    unnamed x4, local copies, waits for them, and re-layouts  6.56 us

profile of v2, /device:TPU:1, one launch (start us, length us, event | category | flops | bytes accessed | tf_op | source)
XLA Modules:
  0.0 159.8 jit_solution(7232766255873388122)
XLA Ops:
  0.6 1.5 copy.9.ids
  2.1 152.6 %step.1 = (f32[4,1024]{1,0:T(4,128)}, bf16[1,128,2048]{2,1,0:T(8,128)(2,1)}, bf16[1,128,2048]{2,1,0:T(8,128)(2,1)}) custom-call(bf16[2,128,1024]{2,1,0:T(8,128)(2,1)} %cell.1, bf16[2,128,1024]{2,1,0:T(8,128)(2,1)} %cot.1, s32[2,128,1]{2,1,0:T(8,128)} %copy.9.ids, bf16[1024,1024]{1,0:T(8,128)(2,1)} %encw.1, bf16[1,1024,2048]{2,1,0:T(8,128)(2,1)} %up_hbm.1, ...), custom_call_target="tpu_custom_call" | custom-call | tf_op jit(solution)/shard_map/step/pallas_call | solution.py:381
  154.7 1.3 copy.13
  156.0 1.9 %copy.14 = bf16[1,128,2048]{2,1,0:T(8,128)(2,1)} copy(bf16[1,128,2048]{2,1,0:T(8,128)(2,1)} %get-tuple-element.7) | data formatting | bytes 1048576
  157.9 1.9 %copy.15 = bf16[1,128,2048]{2,1,0:T(8,128)(2,1)} copy(bf16[1,128,2048]{2,1,0:T(8,128)(2,1)} %get-tuple-element.8) | data formatting | bytes 1048576

commit v3 on v2

--- a/solution.py
+++ b/solution.py
@@ -21,6 +21,7 @@
 SLOT = MICRO * CAP
 SLOTS = N_EX * SLOT
 WIDE = 512
+EARLY = 512
 
 
 def dot(a, b):
@@ -48,13 +49,13 @@
 
 
 def kernel(
-    cell, cot, ids, encw, up_hbm, down_hbm,
+    cell, cot, ids, encw_hbm, up_hbm, down_hbm,
     enc_out, up_out, down_out,
-    w_up, w_down, both, send, recv, pre_grad, active, back, ret,
+    encw, w_up, w_down, normed, send_n, send_g, recv_n, recv_g, pre_grad, active, back, ret,
     enc_s, slope_s, inv_s, placer, fperm, egrad,
-    part, rs_recv, z_recv,
+    part, rs_recv, z_recv, early_recv,
     e_own, e_send, e_recv, x_own, x_send, x_recv, h_own, h_send, h_recv, d_send, d_recv,
-    w_sem, disp_s, disp_r, ret_s, ret_r, rs_s, rs_r, z_s, z_r, c_s, c_r, x_s, x_r, h_s, h_r, d_s, d_r,
+    w_sem, disp_s, disp_r, dispg_s, dispg_r, early_s, early_r, ret_s, ret_r, rs_s, rs_r, z_s, z_r, c_s, c_r, x_s, x_r, h_s, h_r, d_s, d_r,
 ):
     d = lax.axis_index("dp")
     e = lax.axis_index("expert")
@@ -70,6 +71,8 @@
             src_ref=src, dst_ref=dst, send_sem=s, recv_sem=r, device_id=who, device_id_type=MESH
         )
 
+    enc_copy = pltpu.make_async_copy(encw_hbm, encw, w_sem.at[2])
+    enc_copy.start()
     w_copies = [
         pltpu.make_async_copy(up_hbm.at[0], w_up, w_sem.at[0]),
         pltpu.make_async_copy(down_hbm.at[0], w_down, w_sem.at[1]),
@@ -88,53 +91,74 @@
     loop(1, N_EX, greet_expert)
     loop(1, N_DP, greet_dp)
 
-    lower = (
-        lax.broadcasted_iota(jnp.int32, (ROWS, ROWS), 1) < lax.broadcasted_iota(jnp.int32, (ROWS, ROWS), 0)
-    ).astype(BF16)
+    upper = (
+        lax.broadcasted_iota(jnp.int32, (ROWS, ROWS), 0) < lax.broadcasted_iota(jnp.int32, (ROWS, ROWS), 1)
+    ).astype(F32).astype(BF16)
     for m in range(MICRO):
-        label = ids[m]
-        onehot = (label == lax.broadcasted_iota(jnp.int32, (ROWS, 128), 1)).astype(F32)
-        before = dot(lower, onehot.astype(BF16))
-        rank = jnp.sum(before * onehot, axis=1, keepdims=True).astype(jnp.int32)
+        label = ids[m : m + 1, :]
+        onehot = (label == lax.broadcasted_iota(jnp.int32, (N_EX, ROWS), 0)).astype(F32)
+        before = dot(onehot.astype(BF16), upper)
+        rank = jnp.sum(before * onehot, axis=0, keepdims=True).astype(jnp.int32)
         target = label * SLOT + m * CAP + rank
-        slots = lax.broadcasted_iota(jnp.int32, (ROWS, SLOTS), 1)
-        placer[m * ROWS : (m + 1) * ROWS, :] = (slots == target).astype(F32).astype(BF16)
-
-    def encode(i):
-        m, part_row = i // 2, i % 2
-        rows = aligned(part_row, 64)
-        feat = cell[m, rows, :]
-        pre = dot(feat, encw[...])
-        gate = jax.nn.sigmoid(pre)
-        encoded = feat.astype(F32) + pre * gate
-        inverse = lax.rsqrt(jnp.sum(encoded * encoded, axis=1, keepdims=True) * (1.0 / D) + epsilon)
-        out = aligned(i, 64)
-        enc_s[out, :] = encoded
-        slope_s[out, :] = gate * (1.0 + pre * (1.0 - gate))
-        inv_s[out, :] = jnp.broadcast_to(inverse, (64, 128))
-        both[out, :D] = (encoded * inverse).astype(BF16)
-        both[out, D:] = cot[m, rows, :]
-
-    loop(0, 4, encode)
-    pl.semaphore_wait(barrier, N_EX + N_DP - 2)
-
-    def dispatch(c):
-        return copy(send.at[aligned(c, SLOT), :], recv.at[aligned(e, SLOT), :], disp_s.at[c], disp_r.at[e], (d, c))
-
-    def arrival(c):
-        return copy(send.at[aligned(c, SLOT), :], recv.at[aligned(c, SLOT), :], disp_s.at[c], disp_r.at[c], (d, c))
+        slots = lax.broadcasted_iota(jnp.int32, (SLOTS, ROWS), 0)
+        placer[:, m * ROWS : (m + 1) * ROWS] = (slots == target).astype(F32).astype(BF16)
+
+    def to_g(c):
+        return copy(send_g.at[aligned(c, SLOT), :], recv_g.at[aligned(e, SLOT), :], dispg_s.at[c], dispg_r.at[e], (d, c))
+
+    def from_g(c):
+        return copy(send_g.at[aligned(c, SLOT), :], recv_g.at[aligned(c, SLOT), :], dispg_s.at[c], dispg_r.at[c], (d, c))
+
+    def to_n(c):
+        return copy(send_n.at[aligned(c, SLOT), :], recv_n.at[aligned(e, SLOT), :], disp_s.at[c], disp_r.at[e], (d, c))
+
+    def from_n(c):
+        return copy(send_n.at[aligned(c, SLOT), :], recv_n.at[aligned(c, SLOT), :], disp_s.at[c], disp_r.at[c], (d, c))
 
     order = (0, 1, 3, 2)
+    far_first = (1, 3, 2, 0)
 
     def peer(hop, k):
         return ((z_hi + hop) % 4) * 8 + (plane + k) % 8
 
-    for hop in order:
-        h = (z_hi + hop) % 4
-        picks = placer[:, aligned(h, 128)]
-        send[aligned(h, 128), :] = dot_tn(picks, both[...]).astype(BF16)
-        loop(1 if hop == 0 else 0, 8, lambda k: dispatch(peer(hop, k)).start())
-    recv[aligned(e, SLOT), :] = send[aligned(e, SLOT), :]
+    def peers(hop, step):
+        loop(1 if hop == 0 else 0, 8, lambda k: step(peer(hop, k)))
+
+    for hop in far_first:
+        group = aligned((z_hi + hop) % 4, 128)
+        send_g[group, :] = dot(placer[group, :], cot[...]).astype(BF16)
+        if hop == far_first[0]:
+            pl.semaphore_wait(barrier, N_EX + N_DP - 2)
+        peers(hop, lambda c: to_g(c).start())
+    recv_g[aligned(e, SLOT), :] = send_g[aligned(e, SLOT), :]
+
+    inv_s[...] = jnp.zeros_like(inv_s)
+    enc_copy.wait()
+
+    def encode(n):
+        cols = aligned(n, 256)
+        pre = dot(cell[...], encw[:, cols])
+        gate = jax.nn.sigmoid(pre)
+        encoded = cell[:, cols].astype(F32) + pre * gate
+        enc_s[:, cols] = encoded
+        slope_s[:, cols] = gate * (1.0 + pre * (1.0 - gate))
+        square = encoded * encoded
+        inv_s[...] += square[:, :128] + square[:, 128:]
+
+    loop(0, 4, encode)
+
+    def normalize(i):
+        rows = aligned(i, 64)
+        inverse = lax.rsqrt(jnp.sum(inv_s[rows, :], axis=1, keepdims=True) * (1.0 / D) + epsilon)
+        inv_s[rows, :] = jnp.broadcast_to(inverse, (64, 128))
+        normed[rows, :] = (enc_s[rows, :] * inverse).astype(BF16)
+
+    loop(0, 4, normalize)
+    for hop in far_first:
+        group = aligned((z_hi + hop) % 4, 128)
+        send_n[group, :] = dot(placer[group, :], normed[...]).astype(BF16)
+        peers(hop, lambda c: to_n(c).start())
+    recv_n[aligned(e, SLOT), :] = send_n[aligned(e, SLOT), :]
 
     def permute(n):
         col = lax.broadcasted_iota(jnp.int32, (1, 256), 1) + n * 256
@@ -146,8 +170,7 @@
             + ((col >> 9) << 2)
         )
         pick = (lax.broadcasted_iota(jnp.int32, (D, 256), 0) == nat).astype(F32).astype(BF16)
-        for m in range(MICRO):
-            fperm[m * ROWS : (m + 1) * ROWS, aligned(n, 256)] = dot(cell[m], pick).astype(BF16)
+        fperm[:, aligned(n, 256)] = dot(cell[...], pick).astype(BF16)
 
     loop(0, 4, permute)
     for item in w_copies:
@@ -159,34 +182,40 @@
     def came_back(c):
         return copy(back.at[aligned(c, SLOT), :], ret.at[aligned(c, SLOT), :], ret_s.at[c], ret_r.at[c], (d, c))
 
-    for hop in order:
-        h = (z_hi + hop) % 4
-        group = aligned(h, 128)
-        loop(1 if hop == 0 else 0, 8, lambda k: arrival(peer(hop, k)).wait_recv())
+    def mlp(hop):
+        group = aligned((z_hi + hop) % 4, 128)
+        peers(hop, lambda c: from_g(c).wait_recv())
+        peers(hop, lambda c: from_n(c).wait_recv())
 
         def hidden(n):
             cols = aligned(n, WIDE)
-            pre = dot(recv[group, :D], w_up[:, cols])
-            act_grad = dot(recv[group, D:], w_down[:, cols])
+            pre = dot(recv_n[group, :], w_up[:, cols])
+            act_grad = dot(recv_g[group, :], w_down[:, cols])
             gate = jax.nn.sigmoid(pre)
             active[group, cols] = (pre * gate).astype(BF16)
             pre_grad[group, cols] = (act_grad * (gate * (1.0 + pre * (1.0 - gate)))).astype(BF16)
 
         loop(0, H // WIDE, hidden)
 
+    def mlp_back(hop):
+        group = aligned((z_hi + hop) % 4, 128)
+
         def backward(n):
             back[group, aligned(n, 256)] = dot_nt(pre_grad[group, :], w_up[aligned(n, 256), :]).astype(BF16)
 
         loop(0, D // 256, backward)
+
+    for hop in order:
+        mlp(hop)
+        if hop != order[-1]:
+            mlp_back(hop)
         if hop == 0:
-            loop(1, 8, lambda k: give_back(peer(0, k)).start())
-    for hop in order[1:]:
-        loop(0, 8, lambda k: give_back(peer(hop, k)).start())
-    ret[aligned(e, SLOT), :] = back[aligned(e, SLOT), :]
-
-    def grads(p, q, block):
-        up_t = recv[:, aligned(block, 128)].T
-        down_t = recv[:, aligned(block + D // 128, 128)].T
+            peers(0, lambda c: give_back(c).start())
+
+    def grads(p, q):
+        block = ((1 - z_lo) if p == 0 else z_lo) * 4 + (y + (2, 1, 3, 0)[q]) % 4
+        up_t = recv_n[:, aligned(block, 128)].T
+        down_t = recv_g[:, aligned(block, 128)].T
 
         def piece(n):
             cols = aligned(n, WIDE)
@@ -195,31 +224,39 @@
 
         loop(0, H // WIDE, piece)
 
+    late = (pl.ds(EARLY, H - EARLY), pl.ds(0, H))
+
     def rs(p, slot):
         q, which, who = ((0, 0, right), (0, 1, left), (1, 1, right), (2, 0, left), (1, 0, right), (2, 1, left))[slot]
-        return copy(part.at[p, q, which], rs_recv.at[p, slot], rs_s.at[p, slot], rs_r.at[p, slot], who)
+        return copy(
+            part.at[p, q, which, :, late[p]], rs_recv.at[p, slot, :, late[p]], rs_s.at[p, slot], rs_r.at[p, slot], who
+        )
+
+    def early(q, w):
+        return copy(
+            part.at[0, q, w, :, pl.ds(0, EARLY)], early_recv.at[q, w], early_s.at[q, w], early_r.at[q, w], mate
+        )
+
+    def add_early(q):
+        for w in range(2):
+            early(q, w).wait_recv()
+
+            def piece(n):
+                rows = aligned(n, 64)
+                total = part[1, q, w, rows, :EARLY].astype(F32) + early_recv[q, w, rows, :].astype(F32)
+                part[1, q, w, rows, :EARLY] = total.astype(BF16)
+
+            loop(0, 2, piece)
 
     def add_into(p, q, which, others):
         def piece(n):
             rows = aligned(n, 32)
-            total = part[p, q, which, rows, :].astype(F32)
+            total = part[p, q, which, rows, late[p]].astype(F32)
             for slot in others:
-                total = total + rs_recv[p, slot, rows, :].astype(F32)
-            part[p, q, which, rows, :] = total.astype(BF16)
+                total = total + rs_recv[p, slot, rows, late[p]].astype(F32)
+            part[p, q, which, rows, late[p]] = total.astype(BF16)
 
         loop(0, 4, piece)
-
-    for p in range(2):
-        base = ((1 - z_lo) if p == 0 else z_lo) * 4
-        grads(p, 0, base + (y + 2) % 4)
-        rs(p, 0).start()
-        rs(p, 1).start()
-        if p == 0:
-            grads(p, 1, base + (y + 1) % 4)
-            rs(p, 2).start()
-            grads(p, 2, base + (y + 3) % 4)
-            rs(p, 3).start()
-            grads(p, 3, base + y)
 
     def combine(p):
         rs(p, 0).wait_recv()
@@ -229,28 +266,47 @@
         add_into(p, 2, 1, (1,))
         rs(p, 5).start()
 
+    grads(0, 0)
+    rs(0, 0).start()
+    rs(0, 1).start()
+    early(0, 0).start()
+    early(0, 1).start()
+    mlp_back(order[-1])
+    for hop in order[1:]:
+        peers(hop, lambda c: give_back(c).start())
+    ret[aligned(e, SLOT), :] = back[aligned(e, SLOT), :]
+    for q in (1, 2, 3):
+        grads(0, q)
+        if q < 3:
+            rs(0, q + 1).start()
+        early(q, 0).start()
+        early(q, 1).start()
+    grads(1, 0)
     combine(0)
-    base = z_lo * 4
-    grads(1, 1, base + (y + 1) % 4)
+    for q in (1, 2, 3):
+        grads(1, q)
+    add_early(0)
+    rs(1, 0).start()
+    rs(1, 1).start()
+    add_early(1)
     rs(1, 2).start()
-    grads(1, 2, base + (y + 3) % 4)
+    add_early(2)
     rs(1, 3).start()
-    grads(1, 3, base + y)
-
-    loop(1, 8, lambda k: came_back(peer(0, k)).wait_recv())
-    for hop in order[1:]:
-        loop(0, 8, lambda k: came_back(peer(hop, k)).wait_recv())
+    add_early(3)
+
+    for hop in order:
+        peers(hop, lambda c: came_back(c).wait_recv())
 
     def encoder_back(i):
-        rows = aligned(i, 64)
-        norm_grad = dot(placer[rows, :], ret[...])
+        rows = aligned(i, 128)
+        norm_grad = dot_tn(placer[:, rows], ret[...])
         encoded = enc_s[rows, :]
         inverse = inv_s[rows, 0:1]
         mean = jnp.sum(norm_grad * encoded, axis=1, keepdims=True) * (1.0 / D)
         grad = inverse * norm_grad - inverse * inverse * inverse * encoded * mean
         egrad[rows, :] = (grad * slope_s[rows, :]).astype(BF16)
 
-    loop(0, 4, encoder_back)
+    loop(0, 2, encoder_back)
 
     def enc_piece(index):
         return dot(fperm[:, aligned(index, 128)].T, egrad[...])
@@ -295,7 +351,9 @@
         rs(p, 5).wait_recv()
 
     finish(0)
-    to_mate = [copy(part.at[0, 3, w], z_recv.at[w], z_s.at[w], z_r.at[w], mate) for w in range(2)]
+    to_mate = [
+        copy(part.at[0, 3, w, :, late[0]], z_recv.at[w], z_s.at[w], z_r.at[w], mate) for w in range(2)
+    ]
     add_into(0, 3, 0, (3, 4))
     to_mate[0].start()
     add_into(0, 3, 1, (2, 5))
@@ -346,10 +404,11 @@
 
         def piece(n):
             rows = aligned(n, 32)
-            total = part[1, 3, w, rows, :].astype(F32) + z_recv[w, rows, :].astype(F32)
+            total = part[1, 3, w, rows, :].astype(F32)
             for slot in others:
                 total = total + rs_recv[1, slot, rows, :].astype(F32)
-            out[0, rows, :] = total.astype(BF16)
+            out[0, rows, :EARLY] = total[:, :EARLY].astype(BF16)
+            out[0, rows, EARLY:] = (total[:, EARLY:] + z_recv[w, rows, :].astype(F32)).astype(BF16)
 
         loop(0, 4, piece)
 
@@ -360,13 +419,16 @@
     enc_out[...] = total
 
     for hop in order:
-        loop(1 if hop == 0 else 0, 8, lambda k: dispatch(peer(hop, k)).wait_send())
-        loop(1 if hop == 0 else 0, 8, lambda k: give_back(peer(hop, k)).wait_send())
+        peers(hop, lambda c: to_g(c).wait_send())
+        peers(hop, lambda c: to_n(c).wait_send())
+        peers(hop, lambda c: give_back(c).wait_send())
     for p in range(2):
         for slot in range(6):
             rs(p, slot).wait_send()
     for w in range(2):
         to_mate[w].wait_send()
+        for q in range(4):
+            early(q, w).wait_send()
     to_core.wait_send()
     for k in (1, 2, 3):
         x_copy(k).wait_send()
@@ -374,11 +436,17 @@
     loop(1, N_DP, lambda k: d_copy(k).wait_send())
 
 
+def settle(enc_in, up_in, down_in, enc_out, up_out, down_out):
+    enc_out[...] = enc_in[...]
+    up_out[...] = up_in[...]
+    down_out[...] = down_in[...]
+
+
 def body(cell_rows, cotangent, cluster_ids, enc_weight, up_weight, down_weight):
     vmem = pl.BlockSpec(memory_space=pltpu.VMEM)
     hbm = pl.BlockSpec(memory_space=pl.ANY)
     dma = pltpu.SemaphoreType.DMA
-    return pl.pallas_call(
+    outs = pl.pallas_call(
         kernel,
         name="step",
         out_shape=(
@@ -386,14 +454,17 @@
             jax.ShapeDtypeStruct((1, 128, H), BF16),
             jax.ShapeDtypeStruct((1, 128, H), BF16),
         ),
-        in_specs=[vmem, vmem, vmem, vmem, hbm, hbm],
+        in_specs=[vmem, vmem, vmem, hbm, hbm, hbm],
         out_specs=(vmem, vmem, vmem),
         scratch_shapes=[
+            pltpu.VMEM((D, D), BF16),
             pltpu.VMEM((D, H), BF16),
             pltpu.VMEM((D, H), BF16),
-            pltpu.VMEM((ALL_ROWS, 2 * D), BF16),
-            pltpu.VMEM((SLOTS, 2 * D), BF16),
-            pltpu.VMEM((SLOTS, 2 * D), BF16),
+            pltpu.VMEM((ALL_ROWS, D), BF16),
+            pltpu.VMEM((SLOTS, D), BF16),
+            pltpu.VMEM((SLOTS, D), BF16),
+            pltpu.VMEM((SLOTS, D), BF16),
+            pltpu.VMEM((SLOTS, D), BF16),
             pltpu.VMEM((SLOTS, H), BF16),
             pltpu.VMEM((SLOTS, H), BF16),
             pltpu.VMEM((SLOTS, D), BF16),
@@ -401,12 +472,13 @@
             pltpu.VMEM((ALL_ROWS, D), F32),
             pltpu.VMEM((ALL_ROWS, D), F32),
             pltpu.VMEM((ALL_ROWS, 128), F32),
-            pltpu.VMEM((ALL_ROWS, SLOTS), BF16),
+            pltpu.VMEM((SLOTS, ALL_ROWS), BF16),
             pltpu.VMEM((ALL_ROWS, D), BF16),
             pltpu.VMEM((ALL_ROWS, D), BF16),
             pltpu.VMEM((2, 4, 2, 128, H), BF16),
             pltpu.VMEM((2, 6, 128, H), BF16),
-            pltpu.VMEM((2, 128, H), BF16),
+            pltpu.VMEM((2, 128, H - EARLY), BF16),
+            pltpu.VMEM((4, 2, 128, EARLY), BF16),
             pltpu.VMEM((512, D), F32),
             pltpu.VMEM((512, D), BF16),
             pltpu.VMEM((512, D), BF16),
@@ -418,9 +490,13 @@
             pltpu.VMEM((4, 32, D), BF16),
             pltpu.VMEM((N_DP, 4, D), F32),
             pltpu.VMEM((N_DP, 4, D), F32),
-            dma((2,)),
+            dma((3,)),
             dma((N_EX,)),
             dma((N_EX,)),
+            dma((N_EX,)),
+            dma((N_EX,)),
+            dma((4, 2)),
+            dma((4, 2)),
             dma((N_EX,)),
             dma((N_EX,)),
             dma((2, 6)),
@@ -439,7 +515,21 @@
         compiler_params=pltpu.CompilerParams(
             collective_id=0, has_side_effects=True, vmem_limit_bytes=62 << 20
         ),
-    )(cell_rows, cotangent, cluster_ids, enc_weight, up_weight, down_weight)
+    )(
+        cell_rows.reshape(ALL_ROWS, D),
+        cotangent.reshape(ALL_ROWS, D),
+        cluster_ids.reshape(MICRO, ROWS),
+        enc_weight,
+        up_weight,
+        down_weight,
+    )
+    return pl.pallas_call(
+        settle,
+        name="settle",
+        out_shape=tuple(jax.ShapeDtypeStruct(o.shape, o.dtype) for o in outs),
+        in_specs=[vmem] * 3,
+        out_specs=(vmem,) * 3,
+    )(*outs)
 
 
 def solution(mesh):

time: 162 us -> 153 us (0.944); the launches traced: 160 us -> 153 us
  local copies, waits for them, and re-layouts: 6.56 us -> 0 us
    unnamed x4 -> x0, local copies, waits for them, and re-layouts: 6.56 us -> none
    pallas_call x1, Pallas kernels: 153 us -> 150 us  [body(): pl.pallas_call(kernel, name='step', out_shape=(jax.ShapeDtypeStruct((4, D...]
    pallas_call x0 -> x1, Pallas kernels: none -> 2.22 us  [body(): pl.pallas_call(settle, name='settle', out_shape=tuple((jax.ShapeDtypeStru...]
where the time goes in v3:
time: 153 us
  Pallas kernels  152 us (99%)
    pallas_call x1, Pallas kernels, body(): pl.pallas_call(kernel, name='step', out_shape=(jax.ShapeDtypeStruct((4, D...  150 us

profile of v3, /device:TPU:1, one launch (start us, length us, event | category | flops | bytes accessed | tf_op | source)
XLA Modules:
  0.0 152.9 jit_solution(14749151640791431818)
XLA Ops:
  0.6 150.1 %step.1 = (f32[4,1024]{1,0:T(4,128)}, bf16[1,128,2048]{2,1,0:T(8,128)(2,1)}, bf16[1,128,2048]{2,1,0:T(8,128)(2,1)}) custom-call(bf16[256,1024]{1,0:T(8,128)(2,1)} %bitcast.3, bf16[256,1024]{1,0:T(8,128)(2,1)} %bitcast.4, s32[2,128]{1,0:T(2,128)} %bitcast.5, bf16[1024,1024]{1,0:T(8,128)(2,1)} %encw_hbm.1, bf16[1,1024,2048]{2,1,0:T(8,128)(2,1)} %up_hbm.1, ...), custom_call_target="tpu_custom_call" | custom-call | tf_op jit(solution)/shard_map/step/pallas_call | solution.py:449
  150.7 2.2 %settle.1 = (f32[4,1024]{1,0:T(4,128)}, bf16[1,128,2048]{2,1,0:T(8,128)(2,1)}, bf16[1,128,2048]{2,1,0:T(8,128)(2,1)}) custom-call(f32[4,1024]{1,0:T(4,128)} %get-tuple-element.6.enc_in, bf16[1,128,2048]{2,1,0:T(8,128)(2,1)} %get-tuple-element.7.up_in, bf16[1,128,2048]{2,1,0:T(8,128)(2,1)} %get-tuple-element.8.down_in), custom_call_target="tpu_custom_call" | custom-call | tf_op jit(solution)/shard_map/settle/pallas_call | solution.py:526

commit v4 on v3

--- a/solution.py
+++ b/solution.py
@@ -21,7 +21,7 @@
 SLOT = MICRO * CAP
 SLOTS = N_EX * SLOT
 WIDE = 512
-EARLY = 512
+EARLY = 256
 
 
 def dot(a, b):
@@ -186,6 +186,9 @@
         group = aligned((z_hi + hop) % 4, 128)
         peers(hop, lambda c: from_g(c).wait_recv())
         peers(hop, lambda c: from_n(c).wait_recv())
+        if hop == order[-1]:
+            for earlier in order[1:-1]:
+                peers(earlier, lambda c: give_back(c).start())
 
         def hidden(n):
             cols = aligned(n, WIDE)
@@ -269,22 +272,68 @@
     grads(0, 0)
     rs(0, 0).start()
     rs(0, 1).start()
-    early(0, 0).start()
-    early(0, 1).start()
     mlp_back(order[-1])
-    for hop in order[1:]:
-        peers(hop, lambda c: give_back(c).start())
+    peers(order[-1], lambda c: give_back(c).start())
     ret[aligned(e, SLOT), :] = back[aligned(e, SLOT), :]
     for q in (1, 2, 3):
         grads(0, q)
         if q < 3:
             rs(0, q + 1).start()
+    for q in range(4):
         early(q, 0).start()
         early(q, 1).start()
-    grads(1, 0)
     combine(0)
-    for q in (1, 2, 3):
+    for q in range(4):
         grads(1, q)
+
+    for hop in order:
+        peers(hop, lambda c: came_back(c).wait_recv())
+
+    def encoder_back(i):
+        rows = aligned(i, 128)
+        norm_grad = dot_tn(placer[:, rows], ret[...])
+        encoded = enc_s[rows, :]
+        inverse = inv_s[rows, 0:1]
+        mean = jnp.sum(norm_grad * encoded, axis=1, keepdims=True) * (1.0 / D)
+        grad = inverse * norm_grad - inverse * inverse * inverse * encoded * mean
+        egrad[rows, :] = (grad * slope_s[rows, :]).astype(BF16)
+
+    loop(0, 2, encoder_back)
+
+    def enc_piece(index):
+        return dot(fperm[:, aligned(index, 128)].T, egrad[...])
+
+    def enc_other(n):
+        e_send[aligned(n, 128), :] = enc_piece((1 - core) * 4 + n).astype(BF16)
+
+    def enc_own(n):
+        e_own[aligned(n, 128), :] = enc_piece(core * 4 + n)
+
+    loop(0, 4, enc_other)
+    to_core = copy(e_send, e_recv, c_s.at[0], c_r.at[0], (d, e + 1 - 2 * core))
+    to_core.start()
+    loop(0, 4, enc_own)
+
+    to_core.wait_recv()
+
+    def x_device(k):
+        return (x + k) % 4
+
+    def x_copy(k):
+        to = x_device(k)
+        return copy(x_send.at[to], x_recv.at[x], x_s.at[to], x_r.at[x], (d, (z_hi * 4 + to) * 2 + core))
+
+    def x_from(k):
+        to = x_device(k)
+        return copy(x_send.at[to], x_recv.at[to], x_s.at[to], x_r.at[to], (d, (z_hi * 4 + to) * 2 + core))
+
+    for k in (2, 1, 3):
+        rows = aligned(x_device(k), 128)
+        x_send[x_device(k)] = (e_own[rows, :] + e_recv[rows, :].astype(F32)).astype(BF16)
+        x_copy(k).start()
+    rows = aligned(x, 128)
+    x_own[...] = e_own[rows, :] + e_recv[rows, :].astype(F32)
+
     add_early(0)
     rs(1, 0).start()
     rs(1, 1).start()
@@ -294,70 +343,16 @@
     rs(1, 3).start()
     add_early(3)
 
-    for hop in order:
-        peers(hop, lambda c: came_back(c).wait_recv())
-
-    def encoder_back(i):
-        rows = aligned(i, 128)
-        norm_grad = dot_tn(placer[:, rows], ret[...])
-        encoded = enc_s[rows, :]
-        inverse = inv_s[rows, 0:1]
-        mean = jnp.sum(norm_grad * encoded, axis=1, keepdims=True) * (1.0 / D)
-        grad = inverse * norm_grad - inverse * inverse * inverse * encoded * mean
-        egrad[rows, :] = (grad * slope_s[rows, :]).astype(BF16)
-
-    loop(0, 2, encoder_back)
-
-    def enc_piece(index):
-        return dot(fperm[:, aligned(index, 128)].T, egrad[...])
-
-    def enc_other(n):
-        e_send[aligned(n, 128), :] = enc_piece((1 - core) * 4 + n).astype(BF16)
-
-    def enc_own(n):
-        e_own[aligned(n, 128), :] = enc_piece(core * 4 + n)
-
-    loop(0, 4, enc_other)
-    to_core = copy(e_send, e_recv, c_s.at[0], c_r.at[0], (d, e + 1 - 2 * core))
-    to_core.start()
-    loop(0, 4, enc_own)
-
-    combine(1)
-
-    to_core.wait_recv()
-
-    def x_device(k):
-        return (x + k) % 4
-
-    def x_copy(k):
-        to = x_device(k)
-        return copy(x_send.at[to], x_recv.at[x], x_s.at[to], x_r.at[x], (d, (z_hi * 4 + to) * 2 + core))
-
-    def x_from(k):
-        to = x_device(k)
-        return copy(x_send.at[to], x_recv.at[to], x_s.at[to], x_r.at[to], (d, (z_hi * 4 + to) * 2 + core))
-
-    for k in (2, 1, 3):
-        rows = aligned(x_device(k), 128)
-        x_send[x_device(k)] = (e_own[rows, :] + e_recv[rows, :].astype(F32)).astype(BF16)
-        x_copy(k).start()
-    rows = aligned(x, 128)
-    x_own[...] = e_own[rows, :] + e_recv[rows, :].astype(F32)
-
-    def finish(p):
-        rs(p, 3).wait_recv()
-        rs(p, 4).wait_recv()
-        rs(p, 2).wait_recv()
-        rs(p, 5).wait_recv()
-
-    finish(0)
+    def finish(p, w):
+        for slot in ((3, 4), (2, 5))[w]:
+            rs(p, slot).wait_recv()
+
     to_mate = [
         copy(part.at[0, 3, w, :, late[0]], z_recv.at[w], z_s.at[w], z_r.at[w], mate) for w in range(2)
     ]
+    finish(0, 0)
     add_into(0, 3, 0, (3, 4))
     to_mate[0].start()
-    add_into(0, 3, 1, (2, 5))
-    to_mate[1].start()
 
     for k in (1, 3, 2):
         x_from(k).wait_recv()
@@ -381,6 +376,10 @@
         h_send[(z_hi + k) % 4] = x_sum((z_hi + k) % 4).astype(BF16)
         h_copy(k).start()
     h_own[...] = x_sum(z_hi)
+    finish(0, 1)
+    add_into(0, 3, 1, (2, 5))
+    to_mate[1].start()
+    combine(1)
     for k in (1, 3, 2):
         h_from(k).wait_recv()
     total = h_own[...]
@@ -398,9 +397,9 @@
 
     loop(1, N_DP, lambda k: d_copy(k).start())
 
-    finish(1)
     for w, (out, others) in enumerate(((up_out, (3, 4)), (down_out, (2, 5)))):
         to_mate[w].wait_recv()
+        finish(1, w)
 
         def piece(n):
             rows = aligned(n, 32)

time: 153 us -> 138 us (0.902); the launches traced: 153 us -> 136 us
  Pallas kernels: 152 us -> 136 us
    pallas_call x1, Pallas kernels: 150 us -> 133 us  [body(): pl.pallas_call(kernel, name='step', out_shape=(jax.ShapeDtypeStruct((4, D...]
where the time goes in v4:
time: 138 us; the launch traced here: 136 us
  Pallas kernels  136 us (99%)
    pallas_call x1, Pallas kernels, body(): pl.pallas_call(kernel, name='step', out_shape=(jax.ShapeDtypeStruct((4, D...  133 us

profile of v4, /device:TPU:1, one launch (start us, length us, event | category | flops | bytes accessed | tf_op | source)
XLA Modules:
  0.0 136.3 jit_solution(16509951843134308447)
XLA Ops:
  0.6 133.4 %step.1 = (f32[4,1024]{1,0:T(4,128)}, bf16[1,128,2048]{2,1,0:T(8,128)(2,1)}, bf16[1,128,2048]{2,1,0:T(8,128)(2,1)}) custom-call(bf16[256,1024]{1,0:T(8,128)(2,1)} %bitcast.3, bf16[256,1024]{1,0:T(8,128)(2,1)} %bitcast.4, s32[2,128]{1,0:T(2,128)} %bitcast.5, bf16[1024,1024]{1,0:T(8,128)(2,1)} %encw_hbm.1, bf16[1,1024,2048]{2,1,0:T(8,128)(2,1)} %up_hbm.1, ...), custom_call_target="tpu_custom_call" | custom-call | tf_op jit(solution)/shard_map/step/pallas_call | solution.py:448
  134.0 2.2 %settle.1 = (f32[4,1024]{1,0:T(4,128)}, bf16[1,128,2048]{2,1,0:T(8,128)(2,1)}, bf16[1,128,2048]{2,1,0:T(8,128)(2,1)}) custom-call(f32[4,1024]{1,0:T(4,128)} %get-tuple-element.6.enc_in, bf16[1,128,2048]{2,1,0:T(8,128)(2,1)} %get-tuple-element.7.up_in, bf16[1,128,2048]{2,1,0:T(8,128)(2,1)} %get-tuple-element.8.down_in), custom_call_target="tpu_custom_call" | custom-call | tf_op jit(solution)/shard_map/settle/pallas_call | solution.py:525

commit v5 on v4

--- a/solution.py
+++ b/solution.py
@@ -21,7 +21,7 @@
 SLOT = MICRO * CAP
 SLOTS = N_EX * SLOT
 WIDE = 512
-EARLY = 256
+EARLY = 512
 
 
 def dot(a, b):
@@ -51,7 +51,7 @@
 def kernel(
     cell, cot, ids, encw_hbm, up_hbm, down_hbm,
     enc_out, up_out, down_out,
-    encw, w_up, w_down, normed, send_n, send_g, recv_n, recv_g, pre_grad, active, back, ret,
+    encw, w_up, w_down, held, normed, send_n, send_g, recv_n, recv_g, pre_grad, active, back, ret,
     enc_s, slope_s, inv_s, placer, fperm, egrad,
     part, rs_recv, z_recv, early_recv,
     e_own, e_send, e_recv, x_own, x_send, x_recv, h_own, h_send, h_recv, d_send, d_recv,
@@ -82,14 +82,18 @@
 
     barrier = pltpu.get_barrier_semaphore()
 
-    def greet_expert(k):
-        pl.semaphore_signal(barrier, inc=1, device_id=(d, (e + k) % N_EX), device_id_type=MESH)
-
-    def greet_dp(k):
-        pl.semaphore_signal(barrier, inc=1, device_id=((d + k) % N_DP, e), device_id_type=MESH)
-
-    loop(1, N_EX, greet_expert)
-    loop(1, N_DP, greet_dp)
+    def greet_plane(k):
+        index = z_lo * N_EX + e + k
+        who = (((index // N_EX) % 2) * 4 + y, index % N_EX)
+        pl.semaphore_signal(barrier, inc=1, device_id=who, device_id_type=MESH)
+
+    def greet_ring(k):
+        for half in range(2):
+            who = (half * 4 + (y + k) % 4, e)
+            pl.semaphore_signal(barrier, inc=1, device_id=who, device_id_type=MESH)
+
+    loop(1, 2 * N_EX, greet_plane)
+    loop(1, 4, greet_ring)
 
     upper = (
         lax.broadcasted_iota(jnp.int32, (ROWS, ROWS), 0) < lax.broadcasted_iota(jnp.int32, (ROWS, ROWS), 1)
@@ -103,34 +107,67 @@
         slots = lax.broadcasted_iota(jnp.int32, (SLOTS, ROWS), 0)
         placer[:, m * ROWS : (m + 1) * ROWS] = (slots == target).astype(F32).astype(BF16)
 
-    def to_g(c):
-        return copy(send_g.at[aligned(c, SLOT), :], recv_g.at[aligned(e, SLOT), :], dispg_s.at[c], dispg_r.at[e], (d, c))
-
-    def from_g(c):
-        return copy(send_g.at[aligned(c, SLOT), :], recv_g.at[aligned(c, SLOT), :], dispg_s.at[c], dispg_r.at[c], (d, c))
-
-    def to_n(c):
-        return copy(send_n.at[aligned(c, SLOT), :], recv_n.at[aligned(e, SLOT), :], disp_s.at[c], disp_r.at[e], (d, c))
-
-    def from_n(c):
-        return copy(send_n.at[aligned(c, SLOT), :], recv_n.at[aligned(c, SLOT), :], disp_s.at[c], disp_r.at[c], (d, c))
+    def near(hop):
+        return (z_lo, 0, 1 - z_lo, 1)[hop]
+
+    def place(hop):
+        group = (0, 1 + 2 * z_lo, 2, 1 + 2 * z_lo)[hop]
+        return group * 8 + plane
+
+    beside = (z_hi + 3 + 2 * z_lo) % 4
+
+    def source(group, k):
+        half, high = ((z_lo, z_hi), (0, beside), (1 - z_lo, (z_hi + 2) % 4), (1, beside))[group]
+        other = (plane + k) % 8
+        return group * 8 + other, (half * 4 + y, high * 8 + other)
+
+    def target(hop, k):
+        cluster = ((z_hi + hop) % 4) * 8 + (plane + k) % 8
+        return cluster, (near(hop) * 4 + y, cluster)
+
+    def sending(hop, k, src, dst, s, r):
+        cluster, who = target(hop, k)
+        at = place(hop)
+        return copy(src.at[aligned(cluster, SLOT), :], dst.at[aligned(at, SLOT), :], s.at[cluster], r.at[at], who)
+
+    def landing(group, k, src, dst, s, r):
+        at, who = source(group, k)
+        return copy(src.at[aligned(at, SLOT), :], dst.at[aligned(at, SLOT), :], s.at[at], r.at[at], who)
+
+    def to_g(hop, k):
+        return sending(hop, k, send_g, recv_g, dispg_s, dispg_r)
+
+    def from_g(group, k):
+        return landing(group, k, send_g, recv_g, dispg_s, dispg_r)
+
+    def to_n(hop, k):
+        return sending(hop, k, send_n, recv_n, disp_s, disp_r)
+
+    def from_n(group, k):
+        return landing(group, k, send_n, recv_n, disp_s, disp_r)
+
+    def give_back(group, k):
+        at, who = source(group, k)
+        return copy(back.at[aligned(at, SLOT), :], ret.at[aligned(e, SLOT), :], ret_s.at[at], ret_r.at[e], who)
+
+    def came_back(hop, k):
+        cluster, who = target(hop, k)
+        rows = aligned(cluster, SLOT)
+        return copy(back.at[rows, :], ret.at[rows, :], ret_s.at[cluster], ret_r.at[cluster], who)
 
     order = (0, 1, 3, 2)
     far_first = (1, 3, 2, 0)
 
-    def peer(hop, k):
-        return ((z_hi + hop) % 4) * 8 + (plane + k) % 8
-
-    def peers(hop, step):
-        loop(1 if hop == 0 else 0, 8, lambda k: step(peer(hop, k)))
+    def peers(index, step):
+        loop(1 if index == 0 else 0, 8, lambda k: step(index, k))
 
     for hop in far_first:
         group = aligned((z_hi + hop) % 4, 128)
         send_g[group, :] = dot(placer[group, :], cot[...]).astype(BF16)
         if hop == far_first[0]:
-            pl.semaphore_wait(barrier, N_EX + N_DP - 2)
-        peers(hop, lambda c: to_g(c).start())
-    recv_g[aligned(e, SLOT), :] = send_g[aligned(e, SLOT), :]
+            pl.semaphore_wait(barrier, 2 * N_EX - 1 + 6)
+        peers(hop, lambda h, k: to_g(h, k).start())
+    recv_g[aligned(plane, SLOT), :] = send_g[aligned(e, SLOT), :]
 
     inv_s[...] = jnp.zeros_like(inv_s)
     enc_copy.wait()
@@ -157,8 +194,8 @@
     for hop in far_first:
         group = aligned((z_hi + hop) % 4, 128)
         send_n[group, :] = dot(placer[group, :], normed[...]).astype(BF16)
-        peers(hop, lambda c: to_n(c).start())
-    recv_n[aligned(e, SLOT), :] = send_n[aligned(e, SLOT), :]
+        peers(hop, lambda h, k: to_n(h, k).start())
+    recv_n[aligned(plane, SLOT), :] = send_n[aligned(e, SLOT), :]
 
     def permute(n):
         col = lax.broadcasted_iota(jnp.int32, (1, 256), 1) + n * 256
@@ -176,44 +213,56 @@
     for item in w_copies:
         item.wait()
 
-    def give_back(c):
-        return copy(back.at[aligned(c, SLOT), :], ret.at[aligned(e, SLOT), :], ret_s.at[c], ret_r.at[e], (d, c))
-
-    def came_back(c):
-        return copy(back.at[aligned(c, SLOT), :], ret.at[aligned(c, SLOT), :], ret_s.at[c], ret_r.at[c], (d, c))
-
-    def mlp(hop):
-        group = aligned((z_hi + hop) % 4, 128)
-        peers(hop, lambda c: from_g(c).wait_recv())
-        peers(hop, lambda c: from_n(c).wait_recv())
-        if hop == order[-1]:
-            for earlier in order[1:-1]:
-                peers(earlier, lambda c: give_back(c).start())
+    def silu_and_grad(group, cols, act_grad):
+        pre = dot(recv_n[group, :], w_up[:, cols])
+        gate = jax.nn.sigmoid(pre)
+        active[group, cols] = (pre * gate).astype(BF16)
+        pre_grad[group, cols] = (act_grad * (gate * (1.0 + pre * (1.0 - gate)))).astype(BF16)
+
+    def mlp(index):
+        group = pl.ds(index * 128, 128)
+        peers(index, lambda g, k: from_g(g, k).wait_recv())
+        peers(index, lambda g, k: from_n(g, k).wait_recv())
 
         def hidden(n):
             cols = aligned(n, WIDE)
-            pre = dot(recv_n[group, :], w_up[:, cols])
-            act_grad = dot(recv_g[group, :], w_down[:, cols])
-            gate = jax.nn.sigmoid(pre)
-            active[group, cols] = (pre * gate).astype(BF16)
-            pre_grad[group, cols] = (act_grad * (gate * (1.0 + pre * (1.0 - gate)))).astype(BF16)
+            silu_and_grad(group, cols, dot(recv_g[group, :], w_down[:, cols]))
 
         loop(0, H // WIDE, hidden)
 
-    def mlp_back(hop):
-        group = aligned((z_hi + hop) % 4, 128)
+    def mlp_last(index):
+        group = pl.ds(index * 128, 128)
+        peers(index, lambda g, k: from_g(g, k).wait_recv())
+
+        def first(n):
+            cols = aligned(n, WIDE)
+            held[:, cols] = dot(recv_g[group, :], w_down[:, cols])
+
+        loop(0, H // WIDE, first)
+        peers(index, lambda g, k: from_n(g, k).wait_recv())
+        for earlier in order[1:-1]:
+            peers(earlier, lambda g, k: give_back(g, k).start())
+
+        def hidden(n):
+            cols = aligned(n, WIDE)
+            silu_and_grad(group, cols, held[:, cols])
+
+        loop(0, H // WIDE, hidden)
+
+    def mlp_back(index):
+        group = pl.ds(index * 128, 128)
 
         def backward(n):
             back[group, aligned(n, 256)] = dot_nt(pre_grad[group, :], w_up[aligned(n, 256), :]).astype(BF16)
 
         loop(0, D // 256, backward)
 
-    for hop in order:
-        mlp(hop)
-        if hop != order[-1]:
-            mlp_back(hop)
-        if hop == 0:
-            peers(0, lambda c: give_back(c).start())
+    for index in order[:-1]:
+        mlp(index)
+        mlp_back(index)
+        if index == 0:
+            peers(0, lambda g, k: give_back(g, k).start())
+    mlp_last(order[-1])
 
     def grads(p, q):
         block = ((1 - z_lo) if p == 0 else z_lo) * 4 + (y + (2, 1, 3, 0)[q]) % 4
@@ -272,22 +321,27 @@
     grads(0, 0)
     rs(0, 0).start()
     rs(0, 1).start()
+    early(0, 0).start()
+    early(0, 1).start()
     mlp_back(order[-1])
-    peers(order[-1], lambda c: give_back(c).start())
-    ret[aligned(e, SLOT), :] = back[aligned(e, SLOT), :]
+    peers(order[-1], lambda g, k: give_back(g, k).start())
+    ret[aligned(e, SLOT), :] = back[aligned(plane, SLOT), :]
     for q in (1, 2, 3):
         grads(0, q)
         if q < 3:
             rs(0, q + 1).start()
-    for q in range(4):
         early(q, 0).start()
         early(q, 1).start()
     combine(0)
-    for q in range(4):
+    grads(1, 0)
+    add_early(0)
+    rs(1, 0).start()
+    rs(1, 1).start()
+    for q in (1, 2, 3):
         grads(1, q)
 
     for hop in order:
-        peers(hop, lambda c: came_back(c).wait_recv())
+        peers(hop, lambda h, k: came_back(h, k).wait_recv())
 
     def encoder_back(i):
         rows = aligned(i, 128)
@@ -334,9 +388,6 @@
     rows = aligned(x, 128)
     x_own[...] = e_own[rows, :] + e_recv[rows, :].astype(F32)
 
-    add_early(0)
-    rs(1, 0).start()
-    rs(1, 1).start()
     add_early(1)
     rs(1, 2).start()
     add_early(2)
@@ -418,9 +469,9 @@
     enc_out[...] = total
 
     for hop in order:
-        peers(hop, lambda c: to_g(c).wait_send())
-        peers(hop, lambda c: to_n(c).wait_send())
-        peers(hop, lambda c: give_back(c).wait_send())
+        peers(hop, lambda h, k: to_g(h, k).wait_send())
+        peers(hop, lambda h, k: to_n(h, k).wait_send())
+        peers(hop, lambda g, k: give_back(g, k).wait_send())
     for p in range(2):
         for slot in range(6):
             rs(p, slot).wait_send()
@@ -459,6 +510,7 @@
             pltpu.VMEM((D, D), BF16),
             pltpu.VMEM((D, H), BF16),
             pltpu.VMEM((D, H), BF16),
+            pltpu.VMEM((ROWS, H), F32),
             pltpu.VMEM((ALL_ROWS, D), BF16),
             pltpu.VMEM((SLOTS, D), BF16),
             pltpu.VMEM((SLOTS, D), BF16),

time: 138 us -> 133 us (0.964)
  Pallas kernels: 136 us -> 130 us
    pallas_call x1, Pallas kernels: 133 us -> 128 us  [body(): pl.pallas_call(kernel, name='step', out_shape=(jax.ShapeDtypeStruct((4, D...]
where the time goes in v5:
time: 133 us; the launch traced here: 131 us
  Pallas kernels  130 us (98%)
    pallas_call x1, Pallas kernels, body(): pl.pallas_call(kernel, name='step', out_shape=(jax.ShapeDtypeStruct((4, D...  128 us

profile of v5, /device:TPU:1, one launch (start us, length us, event | category | flops | bytes accessed | tf_op | source)
XLA Modules:
  0.0 131.0 jit_solution(3180773102646107809)
XLA Ops:
  0.6 128.2 %step.1 = (f32[4,1024]{1,0:T(4,128)}, bf16[1,128,2048]{2,1,0:T(8,128)(2,1)}, bf16[1,128,2048]{2,1,0:T(8,128)(2,1)}) custom-call(bf16[256,1024]{1,0:T(8,128)(2,1)} %bitcast.3, bf16[256,1024]{1,0:T(8,128)(2,1)} %bitcast.4, s32[2,128]{1,0:T(2,128)} %bitcast.5, bf16[1024,1024]{1,0:T(8,128)(2,1)} %encw_hbm.1, bf16[1,1024,2048]{2,1,0:T(8,128)(2,1)} %up_hbm.1, ...), custom_call_target="tpu_custom_call" | custom-call | tf_op jit(solution)/shard_map/step/pallas_call | solution.py:499
  128.8 2.2 %settle.1 = (f32[4,1024]{1,0:T(4,128)}, bf16[1,128,2048]{2,1,0:T(8,128)(2,1)}, bf16[1,128,2048]{2,1,0:T(8,128)(2,1)}) custom-call(f32[4,1024]{1,0:T(4,128)} %get-tuple-element.6.enc_in, bf16[1,128,2048]{2,1,0:T(8,128)(2,1)} %get-tuple-element.7.up_in, bf16[1,128,2048]{2,1,0:T(8,128)(2,1)} %get-tuple-element.8.down_in), custom_call_target="tpu_custom_call" | custom-call | tf_op jit(solution)/shard_map/settle/pallas_call | solution.py:577

commit v6 on v5

--- a/solution.py
+++ b/solution.py
@@ -21,7 +21,7 @@
 SLOT = MICRO * CAP
 SLOTS = N_EX * SLOT
 WIDE = 512
-EARLY = 512
+EARLY = 384
 
 
 def dot(a, b):
@@ -198,16 +198,16 @@
     recv_n[aligned(plane, SLOT), :] = send_n[aligned(e, SLOT), :]
 
     def permute(n):
-        col = lax.broadcasted_iota(jnp.int32, (1, 256), 1) + n * 256
+        row = lax.broadcasted_iota(jnp.int32, (256, 1), 0) + n * 256
         nat = (
-            (col & 3)
-            + (((col >> 2) & 7) << 7)
-            + (((col >> 5) & 3) << 5)
-            + (((col >> 7) & 3) << 3)
-            + ((col >> 9) << 2)
+            (row & 3)
+            + (((row >> 2) & 7) << 7)
+            + (((row >> 5) & 3) << 5)
+            + (((row >> 7) & 3) << 3)
+            + ((row >> 9) << 2)
         )
-        pick = (lax.broadcasted_iota(jnp.int32, (D, 256), 0) == nat).astype(F32).astype(BF16)
-        fperm[:, aligned(n, 256)] = dot(cell[...], pick).astype(BF16)
+        pick = (lax.broadcasted_iota(jnp.int32, (256, D), 1) == nat).astype(F32).astype(BF16)
+        fperm[aligned(n, 256), :] = dot_nt(pick, cell[...]).astype(BF16)
 
     loop(0, 4, permute)
     for item in w_copies:
@@ -355,7 +355,7 @@
     loop(0, 2, encoder_back)
 
     def enc_piece(index):
-        return dot(fperm[:, aligned(index, 128)].T, egrad[...])
+        return dot(fperm[aligned(index, 128), :], egrad[...])
 
     def enc_other(n):
         e_send[aligned(n, 128), :] = enc_piece((1 - core) * 4 + n).astype(BF16)
@@ -392,7 +392,6 @@
     rs(1, 2).start()
     add_early(2)
     rs(1, 3).start()
-    add_early(3)
 
     def finish(p, w):
         for slot in ((3, 4), (2, 5))[w]:
@@ -404,6 +403,7 @@
     finish(0, 0)
     add_into(0, 3, 0, (3, 4))
     to_mate[0].start()
+    combine(1)
 
     for k in (1, 3, 2):
         x_from(k).wait_recv()
@@ -430,7 +430,6 @@
     finish(0, 1)
     add_into(0, 3, 1, (2, 5))
     to_mate[1].start()
-    combine(1)
     for k in (1, 3, 2):
         h_from(k).wait_recv()
     total = h_own[...]
@@ -449,6 +448,7 @@
     loop(1, N_DP, lambda k: d_copy(k).start())
 
     for w, (out, others) in enumerate(((up_out, (3, 4)), (down_out, (2, 5)))):
+        early(3, w).wait_recv()
         to_mate[w].wait_recv()
         finish(1, w)
 
@@ -457,7 +457,7 @@
             total = part[1, 3, w, rows, :].astype(F32)
             for slot in others:
                 total = total + rs_recv[1, slot, rows, :].astype(F32)
-            out[0, rows, :EARLY] = total[:, :EARLY].astype(BF16)
+            out[0, rows, :EARLY] = (total[:, :EARLY] + early_recv[3, w, rows, :].astype(F32)).astype(BF16)
             out[0, rows, EARLY:] = (total[:, EARLY:] + z_recv[w, rows, :].astype(F32)).astype(BF16)
 
         loop(0, 4, piece)
@@ -524,7 +524,7 @@
             pltpu.VMEM((ALL_ROWS, D), F32),
             pltpu.VMEM((ALL_ROWS, 128), F32),
             pltpu.VMEM((SLOTS, ALL_ROWS), BF16),
-            pltpu.VMEM((ALL_ROWS, D), BF16),
+            pltpu.VMEM((D, ALL_ROWS), BF16),
             pltpu.VMEM((ALL_ROWS, D), BF16),
             pltpu.VMEM((2, 4, 2, 128, H), BF16),
             pltpu.VMEM((2, 6, 128, H), BF16),

time: 133 us -> 136 us (1.023)
  Pallas kernels: 130 us -> 133 us
    pallas_call x1, Pallas kernels: 128 us -> 131 us  [body(): pl.pallas_call(kernel, name='step', out_shape=(jax.ShapeDtypeStruct((4, D...]
where the time goes in v6:
time: 136 us; the launch traced here: 134 us
  Pallas kernels  133 us (98%)
    pallas_call x1, Pallas kernels, body(): pl.pallas_call(kernel, name='step', out_shape=(jax.ShapeDtypeStruct((4, D...  131 us

profile of v6, /device:TPU:1, one launch (start us, length us, event | category | flops | bytes accessed | tf_op | source)
XLA Modules:
  0.0 133.6 jit_solution(2028406939330825506)
XLA Ops:
  0.6 130.8 %step.1 = (f32[4,1024]{1,0:T(4,128)}, bf16[1,128,2048]{2,1,0:T(8,128)(2,1)}, bf16[1,128,2048]{2,1,0:T(8,128)(2,1)}) custom-call(bf16[256,1024]{1,0:T(8,128)(2,1)} %bitcast.3, bf16[256,1024]{1,0:T(8,128)(2,1)} %bitcast.4, s32[2,128]{1,0:T(2,128)} %bitcast.5, bf16[1024,1024]{1,0:T(8,128)(2,1)} %encw_hbm.1, bf16[1,1024,2048]{2,1,0:T(8,128)(2,1)} %up_hbm.1, ...), custom_call_target="tpu_custom_call" | custom-call | tf_op jit(solution)/shard_map/step/pallas_call | solution.py:499
  131.4 2.2 %settle.1 = (f32[4,1024]{1,0:T(4,128)}, bf16[1,128,2048]{2,1,0:T(8,128)(2,1)}, bf16[1,128,2048]{2,1,0:T(8,128)(2,1)}) custom-call(f32[4,1024]{1,0:T(4,128)} %get-tuple-element.6.enc_in, bf16[1,128,2048]{2,1,0:T(8,128)(2,1)} %get-tuple-element.7.up_in, bf16[1,128,2048]{2,1,0:T(8,128)(2,1)} %get-tuple-element.8.down_in), custom_call_target="tpu_custom_call" | custom-call | tf_op jit(solution)/shard_map/settle/pallas_call | solution.py:577

commit v7 on v6

--- a/solution.py
+++ b/solution.py
@@ -21,7 +21,7 @@
 SLOT = MICRO * CAP
 SLOTS = N_EX * SLOT
 WIDE = 512
-EARLY = 384
+EARLY = 640
 
 
 def dot(a, b):

time: 136 us -> 133 us (0.978); the launches traced: 134 us -> 133 us
  no operation moved by 1% of the time
where the time goes in v7:
time: 133 us
  Pallas kernels  132 us (99%)
    pallas_call x1, Pallas kernels, body(): pl.pallas_call(kernel, name='step', out_shape=(jax.ShapeDtypeStruct((4, D...  130 us

profile of v7, /device:TPU:1, one launch (start us, length us, event | category | flops | bytes accessed | tf_op | source)
XLA Modules:
  0.0 132.9 jit_solution(6550757132044425285)
XLA Ops:
  0.6 130.0 %step.1 = (f32[4,1024]{1,0:T(4,128)}, bf16[1,128,2048]{2,1,0:T(8,128)(2,1)}, bf16[1,128,2048]{2,1,0:T(8,128)(2,1)}) custom-call(bf16[256,1024]{1,0:T(8,128)(2,1)} %bitcast.3, bf16[256,1024]{1,0:T(8,128)(2,1)} %bitcast.4, s32[2,128]{1,0:T(2,128)} %bitcast.5, bf16[1024,1024]{1,0:T(8,128)(2,1)} %encw_hbm.1, bf16[1,1024,2048]{2,1,0:T(8,128)(2,1)} %up_hbm.1, ...), custom_call_target="tpu_custom_call" | custom-call | tf_op jit(solution)/shard_map/step/pallas_call | solution.py:499
  130.7 2.2 %settle.1 = (f32[4,1024]{1,0:T(4,128)}, bf16[1,128,2048]{2,1,0:T(8,128)(2,1)}, bf16[1,128,2048]{2,1,0:T(8,128)(2,1)}) custom-call(f32[4,1024]{1,0:T(4,128)} %get-tuple-element.6.enc_in, bf16[1,128,2048]{2,1,0:T(8,128)(2,1)} %get-tuple-element.7.up_in, bf16[1,128,2048]{2,1,0:T(8,128)(2,1)} %get-tuple-element.8.down_in), custom_call_target="tpu_custom_call" | custom-call | tf_op jit(solution)/shard_map/settle/pallas_call | solution.py:577
